TPU v7x, 32 devices: a whole 2x2x4 slice. The times are simulated.
32 devices in a mesh: rows: 2 (over core), waves: 16 (over z, y, x).
Axes of the slice: x: 2, y: 2, z: 4, core: 2. Of those that a mesh axis runs over, the one named last changes fastest.
Arguments:
- feats: float32 [8192, 256], P(('rows', 'waves')), may hold values from -6 to 6
- positions: float32 [3, 8192], P(None, ('rows', 'waves')), may hold values from 0 to 6
- cell_counts: int32 [64], P(('rows', 'waves')), may hold values from 1 to 128
- neighbours: int32 [64, 5], P(('rows', 'waves')), may hold values from 0 to 63, as said below
- nbr_count: int32 [64], P(('rows', 'waves')), may hold values from 3 to 5
- kvec: float32 [3, 3072], P(None, 'waves'), may hold values from -4 to 4
- filters: float32 [3072, 256], P('waves'), may hold values from -5 to 5
- w_msg: float32 [256, 256], replicated, may hold values from -0.375 to 0.375
- w_val: float32 [256, 256], replicated, may hold values from -0.375 to 0.375
- w_one: float32 [256, 256], replicated, may hold values from -0.375 to 0.375
- w_two: float32 [256, 256], replicated, may hold values from -0.375 to 0.375
Outputs:
- updated: float32 [8192, 256], P(('rows', 'waves'))
Inputs may be any that keep to these rules, and one draw needn't show every extreme that they name: `neighbours`: column 0 of each cell's list is the cell itself, column 1 the cell (c - 2) mod 64, column 2 the cell (c + 2) mod 64; the 5 entries of a list are distinct cells, and every listed cell c' of cell c satisfies (c' - c) mod 64 <= 2 or (c - c') mod 64 <= 2; entries at or beyond nbr_count are in range and unused.
All inputs are finite; a program needn't handle non-finite values.
Results may differ from a plain program's by a relative error of at most 0.0003.
Values sent between devices are 32-bit elements; how exact they have to be, the bound alone decides.
A program may use at most 128 MiB of HBM per device.

v0:
```python
import functools
import math

import jax
import jax.numpy as jnp
from jax import lax
from jax.experimental import pallas as pl
from jax.experimental.pallas import tpu as pltpu
from jax.sharding import PartitionSpec as P

MESH = pl.DeviceIdType.MESH
F32 = jnp.float32
BF16 = jnp.bfloat16

SIN = (6.283185302511498, -41.341700405316864, 81.60513138577438, -76.7030153535419, 42.02592698387571, -14.899846661980089, 3.238137503130986)
COS = (0.9999999890590201, -19.739204499453688, 64.93911745988827, -85.45013953077586, 60.16763095018129, -25.96759924584206, 6.528658157862129)


def split(x):
    high = x.astype(BF16)
    return high, (x - high.astype(F32)).astype(BF16)


def mm(a, b):
    return jnp.dot(a, b, preferred_element_type=F32)


def dot3(a, b):
    return mm(a[0], b[0]) + mm(a[0], b[1]) + mm(a[1], b[0])


def sincos(turns):
    x = turns - jnp.floor(turns + 0.5)
    y = x * x
    s = jnp.full_like(y, SIN[-1])
    for coefficient in SIN[-2::-1]:
        s = s * y + coefficient
    c = jnp.full_like(y, COS[-1])
    for coefficient in COS[-2::-1]:
        c = c * y + coefficient
    return s * x, c


def columns(rows):
    height, width = rows.shape
    return jnp.concatenate([rows, jnp.zeros((128 - height, width), F32)], axis=0).T


def body(
    nz, plane, scale,
    counts, neigh, ncount, feats, pos, kv, filt, w_msg, w_val, w_one, w_two,
    out,
    feats_all, pos_all, kv_all, k_cols, ch, cl, sh, sl, fbh, fbl,
    s_acc, xbuf, zs, zr, f_all, fth, ftl, es, er, msg,
    s_pos, r_pos, s_feat, r_feat, s_kv, r_kv, s_x, r_x, s_z, r_z, s_f, r_f, s_g, s_e, r_e,
):
    slots, width = feats.shape
    kb = filt.shape[0]
    half = kb // 2
    kall = nz * kb
    kpad = k_cols.shape[0]
    cells = counts.shape[0]
    cell = slots // cells
    waves = nz * plane
    r = lax.axis_index("rows")
    w = lax.axis_index("waves")
    z = w // plane
    p = w % plane
    other = (1 - r, w)
    at_low = p == 0
    at_high = p == plane - 1
    edge_w = jnp.where(at_low, (w + waves - 1) % waves, (w + 1) % waves)
    crosses = jnp.where(at_low, z == 0, z == nz - 1)
    edge_r = jnp.where(crosses, 1 - r, r)
    edge = (edge_r, edge_w)

    def plane_dev(j):
        return (r, z * plane + (p + j) % plane)

    def z_dev(j):
        return (r, ((z + j) % nz) * plane + p)

    def rcopy(src, dst, ssem, rsem, dev):
        return pltpu.make_async_remote_copy(
            src_ref=src, dst_ref=dst, send_sem=ssem, recv_sem=rsem, device_id=dev, device_id_type=MESH
        )

    def rows_of(block):
        return pl.ds(pl.multiple_of(block * slots, slots), slots)

    barrier = pltpu.get_barrier_semaphore()
    pl.semaphore_signal(barrier, inc=1, device_id=other, device_id_type=MESH)
    for j in range(1, nz):
        pl.semaphore_signal(barrier, inc=1, device_id=z_dev(j), device_id_type=MESH)

    @pl.loop(1, plane)
    def _(j):
        pl.semaphore_signal(barrier, inc=1, device_id=plane_dev(j), device_id_type=MESH)

    @pl.when(at_low | at_high)
    def _():
        pl.semaphore_signal(barrier, inc=1, device_id=edge, device_id_type=MESH)

    pl.semaphore_wait(barrier, nz + plane - 1 + jnp.where(at_low | at_high, 1, 0))

    def kv_copy(j):
        return rcopy(kv, kv_all.at[z], s_kv.at[j], r_kv.at[z], z_dev(j))

    def kv_arrival(j):
        q = (z + j) % nz
        return rcopy(kv, kv_all.at[q], s_kv.at[j], r_kv.at[q], z_dev(j))

    def pos_copy(j):
        return rcopy(pos, pos_all.at[p], s_pos.at[j], r_pos.at[p], plane_dev(j))

    def pos_arrival(q):
        return rcopy(pos, pos_all.at[q], s_pos.at[0], r_pos.at[q], other)

    def feat_copy(j):
        return rcopy(feats, feats_all.at[p], s_feat.at[j], r_feat.at[p], plane_dev(j))

    def feat_arrival(q):
        return rcopy(feats, feats_all.at[q], s_feat.at[0], r_feat.at[q], other)

    edge_pos = rcopy(pos, pos_all.at[plane], s_pos.at[0], r_pos.at[plane], edge)
    edge_feat = rcopy(feats, feats_all.at[plane], s_feat.at[0], r_feat.at[plane], edge)

    for j in range(1, nz):
        kv_copy(j).start()

    @pl.loop(1, plane)
    def _(j):
        pos_copy(j).start()

    @pl.loop(1, plane)
    def _(j):
        feat_copy(j).start()

    @pl.when(at_low | at_high)
    def _():
        edge_pos.start()
        edge_feat.start()

    def place_k(block, rows):
        k_cols[pl.ds(pl.multiple_of(block * kb, 8), kb), :] = columns(rows)[:kb]

    place_k(z, kv[...])
    if kpad > kall:
        k_cols[kall:, :] = jnp.zeros((kpad - kall, 128), F32)
    for j in range(1, nz):
        kv_arrival(j).wait_recv()
        q = (z + j) % nz
        place_k(q, kv_all[q])

    chunk = 32

    def phases(q, rows3):
        px, py, pz = rows3[0:1], rows3[1:2], rows3[2:3]
        lanes = rows_of(q)

        @pl.loop(0, kpad // chunk)
        def _(i):
            ks = pl.ds(pl.multiple_of(i * chunk, chunk), chunk)
            kc = k_cols[ks, :]
            s, c = sincos(kc[:, 0:1] * px + kc[:, 1:2] * py + kc[:, 2:3] * pz)
            a, b = split(c)
            ch[ks, lanes] = a
            cl[ks, lanes] = b
            a, b = split(s)
            sh[ks, lanes] = a
            sl[ks, lanes] = b

    def place_f(q, block):
        a, b = split(block)
        fbh[rows_of(q), :] = a
        fbl[rows_of(q), :] = b

    phases(p, pos[...])
    place_f(p, feats[...])

    @pl.loop(1, plane)
    def _(j):
        q = (p + j) % plane
        pos_arrival(q).wait_recv()
        phases(q, pos_all[q])

    @pl.loop(1, plane)
    def _(j):
        q = (p + j) % plane
        feat_arrival(q).wait_recv()
        place_f(q, feats_all[q])

    natoms = plane * slots

    def partial_sums(zb):
        ks = pl.ds(pl.multiple_of(zb * kb, 8), kb)
        f = (fbh[:natoms, :], fbl[:natoms, :])
        for part, (hi, lo) in enumerate(((ch, cl), (sh, sl))):
            total = dot3((hi[ks, :], lo[ks, :]), f)
            for h in range(2):
                s_acc[zb, h, part] = total[h * half : (h + 1) * half]

    def x_copy(zb):
        return rcopy(s_acc.at[zb, 1 - r], xbuf.at[zb], s_x.at[zb], r_x.at[zb], other)

    def step(up):
        return z_dev(1) if up else z_dev(nz - 1)

    def s_hop(zb, up):
        side = 0 if up else 1
        return rcopy(zs.at[zb], zr.at[side, zb], s_z.at[zb], r_z.at[side, zb], step(up))

    def pass_on(zb):
        x_copy(zb).wait_recv()
        zs[zb] = s_acc[zb, r] + xbuf[zb]
        for up, ahead, behind in ((True, z < zb, z > 0), (False, z > zb, z < nz - 1)):

            @pl.when(ahead & behind)
            def _():
                s_hop(zb, up).wait_recv()
                zs[zb] = zs[zb] + zr[0 if up else 1, zb]

            @pl.when(ahead)
            def _():
                s_hop(zb, up).start()

    order = []
    for i in range(nz // 2):
        order += [nz - 1 - i, i]
    for i, zb in enumerate(order):
        partial_sums(zb)
        x_copy(zb).start()
        if i:
            pass_on(order[i - 1])
    pass_on(order[-1])

    @pl.when(at_low | at_high)
    def _():
        edge_pos.wait_recv()
        edge_feat.wait_recv()
        place_f(plane, feats_all[plane])

    first = (r * waves + w) * cells
    total_cells = cells * waves * 2
    own_cols = columns(pos[...])
    low_slot = jnp.where(at_low, plane, p - 1)
    high_slot = jnp.where(at_high, plane, p + 1)
    same = lax.broadcasted_iota(jnp.int32, (slots, slots), 0) == lax.broadcasted_iota(
        jnp.int32, (slots, slots), 1
    )
    row_cell = lax.broadcasted_iota(jnp.int32, (slots, slots), 0) // cell
    col_cell = lax.broadcasted_iota(jnp.int32, (slots, slots), 1) // cell

    def listed(c, target):
        found = jnp.float32(0.0)
        for b in range(neigh.shape[1]):
            hit = (neigh[c, b] == target) & (b < ncount[c])
            found = found + jnp.where(hit, 1.0, 0.0)
        return found

    gathered = jnp.zeros((slots, width), F32)
    for shift, slot in ((-1, low_slot), (0, p), (1, high_slot)):
        near = pos[...] if shift == 0 else pos_all[slot]
        dist = jnp.zeros((slots, slots), F32)
        for axis in range(3):
            diff = own_cols[:, axis : axis + 1] - near[axis : axis + 1]
            dist = dist + diff * diff
        live = jnp.zeros((slots, slots), F32)
        for c in range(cells):
            for t in range(cells):
                target = (first + shift * cells + t + total_cells) % total_cells
                live = jnp.where((row_cell == c) & (col_cell == t), listed(c, target), live)
        weight = jnp.exp(-0.125 * dist) * live
        if shift == 0:
            weight = jnp.where(same, 0.0, weight)
        gathered = gathered + dot3(split(weight), (fbh[rows_of(slot), :], fbl[rows_of(slot), :]))
    msg[...] = feats[...] + 0.125 * dot3(split(gathered), split(w_msg[...]))

    for up, behind in ((True, z > 0), (False, z < nz - 1)):

        @pl.when(behind)
        def _():
            s_hop(z, up).wait_recv()
            zs[z] = zs[z] + zr[0 if up else 1, z]

    total = zs[z]
    mine = pl.multiple_of(r * half, 8)
    wv = split(w_val[...])
    own_filter = filt[pl.ds(mine, half), :] * scale

    hw = width // 2

    def share(fh, zb, h):
        return f_all.at[fh, :, pl.ds(pl.multiple_of((zb * 2 + h) * half, 8), half), :]

    for part in range(2):
        filtered = own_filter * dot3(split(total[part]), wv)
        for fh in range(2):
            f_all[fh, part, pl.ds(pl.multiple_of((z * 2 + r) * half, 8), half), :] = filtered[
                :, fh * hw : (fh + 1) * hw
            ]
    if kpad > kall:
        f_all[:, :, kall:, :] = jnp.zeros((2, 2, kpad - kall, hw), F32)

    def f_hop(fh, zb, up, d):
        here = share(fh, zb, r)
        return rcopy(here, here, s_f.at[fh, int(up), d], r_f.at[fh, zb, r], step(up))

    def f_relay(fh, zb):
        here = share(fh, zb, r)
        return rcopy(here, here, s_g.at[fh, zb], r_f.at[fh, zb, r], other)

    def f_arrival(fh, zb, h):
        here = share(fh, zb, h)
        return rcopy(here, here, s_g.at[fh, zb], r_f.at[fh, zb, h], other)

    def f_own(fh):
        for up, ahead in ((True, z < nz - 1), (False, z > 0)):

            @pl.when(ahead)
            def _():
                f_hop(fh, z, up, 0).start()

        f_relay(fh, z).start()

    def f_pass(fh, d):
        for up, there, ahead in ((True, z >= d, z < nz - 1), (False, z + d < nz, z > 0)):
            zb = z - d if up else z + d

            @pl.when(there)
            def _():
                f_arrival(fh, zb, r).wait_recv()

            @pl.when(there & ahead)
            def _():
                f_hop(fh, zb, up, d).start()

            @pl.when(there)
            def _():
                f_relay(fh, zb).start()

    def back(fh, q):
        lanes = rows_of(q)
        return dot3((fth[fh, 0], ftl[fh, 0]), (ch[:, lanes], cl[:, lanes])) + dot3(
            (fth[fh, 1], ftl[fh, 1]), (sh[:, lanes], sl[:, lanes])
        )

    def e_copy(fh, j):
        return rcopy(es.at[fh, j], er.at[fh, j], s_e.at[fh, j], r_e.at[fh, j], plane_dev(j))

    def gather_half(fh):
        for zb in range(nz):
            f_arrival(fh, zb, 1 - r).wait_recv()
        for part in range(2):
            a, b = split(f_all[fh, part].T)
            fth[fh, part] = a
            ftl[fh, part] = b

    def back_range(fh, start, stop):
        @pl.loop(start, stop)
        def _(j):
            es[fh, j] = back(fh, (p + j) % plane)
            e_copy(fh, j).start()

    f_own(0)
    for d in range(1, nz):
        f_pass(0, d)
        if d == 1:
            f_own(1)
    gather_half(0)
    cuts = [1 + d * (plane - 1) // (nz - 1) for d in range(nz)]
    for d in range(1, nz):
        f_pass(1, d)
        back_range(0, cuts[d - 1], cuts[d])
    gather_half(1)
    back_range(1, 1, plane)
    for fh in range(2):
        es[fh, 0] = back(fh, p)

    for fh in range(2):

        @pl.loop(1, plane)
        def _(j):
            e_copy(fh, j).wait_recv()
            es[fh, 0] = es[fh, 0] + er[fh, j]

    summed = msg[...] + jnp.concatenate([es[0, 0].T, es[1, 0].T], axis=1)
    normed = summed / jnp.sqrt(jnp.mean(summed * summed, axis=1, keepdims=True) + 1e-06)
    v = dot3(split(normed), split(w_one[...]))
    hidden = v / (1.0 + jnp.exp(-v))
    result = summed + dot3(split(hidden), split(w_two[...]))
    slot_ids = lax.broadcasted_iota(jnp.int32, (cell, width), 0)
    for c in range(cells):
        out[c * cell : (c + 1) * cell, :] = jnp.where(
            slot_ids < counts[c], result[c * cell : (c + 1) * cell], 0.0
        )

    for j in range(1, nz):
        kv_copy(j).wait_send()
    for zb in range(nz):
        x_copy(zb).wait_send()
        for up, ahead in ((True, z < zb), (False, z > zb)):

            @pl.when(ahead)
            def _():
                s_hop(zb, up).wait_send()

        for fh in range(2):
            f_relay(fh, zb).wait_send()
    for fh in range(2):
        for d in range(nz):
            for up, there, ahead in ((True, z >= d, z < nz - 1), (False, z + d < nz, z > 0)):

                @pl.when(there & ahead)
                def _():
                    f_hop(fh, z - d if up else z + d, up, d).wait_send()

    @pl.loop(1, plane)
    def _(j):
        pos_copy(j).wait_send()
        feat_copy(j).wait_send()
        for fh in range(2):
            e_copy(fh, j).wait_send()

    @pl.when(at_low | at_high)
    def _():
        edge_pos.wait_send()
        edge_feat.wait_send()


def shards(
    nz, feats, positions, cell_counts, neighbours, nbr_count, kvec, filters, w_msg, w_val, w_one, w_two
):
    cells = cell_counts.shape[0]
    slots, width = feats.shape
    cell = slots // cells
    kb = kvec.shape[1]
    waves = lax.axis_size("waves")
    plane = waves // nz
    devices = lax.axis_size("rows") * waves
    kpad = -(-nz * kb // 128) * 128
    kbpad = -(-kb // 128) * 128
    half = kb // 2
    scale = 1.0 / math.sqrt(float(slots * devices) * float(kb * waves))
    slot_ids = jnp.arange(cell, dtype=jnp.int32)
    valid = (slot_ids[None, :] < cell_counts[:, None]).astype(F32).reshape(-1)
    masked = feats * valid[:, None]
    pos8 = jnp.pad(positions, ((0, 5), (0, 0)))
    kv8 = jnp.pad(kvec * (0.5 / math.pi), ((0, 5), (0, kbpad - kb)))
    natoms = plane * slots
    vm = pltpu.VMEM
    dma = pltpu.SemaphoreType.DMA
    smem_spec = pl.BlockSpec(memory_space=pltpu.SMEM)
    vmem_spec = pl.BlockSpec(memory_space=pltpu.VMEM)
    return pl.pallas_call(
        functools.partial(body, nz, plane, scale),
        out_shape=jax.ShapeDtypeStruct((slots, width), F32),
        in_specs=[smem_spec] * 3 + [vmem_spec] * 8,
        out_specs=vmem_spec,
        scratch_shapes=[
            vm((plane + 1, slots, width), F32),
            vm((plane + 1, 8, slots), F32),
            vm((nz, 8, kbpad), F32),
            vm((kpad, 128), F32),
            vm((kpad, natoms), BF16),
            vm((kpad, natoms), BF16),
            vm((kpad, natoms), BF16),
            vm((kpad, natoms), BF16),
            vm((natoms + slots, width), BF16),
            vm((natoms + slots, width), BF16),
            vm((nz, 2, 2, half, width), F32),
            vm((nz, 2, half, width), F32),
            vm((nz, 2, half, width), F32),
            vm((2, nz, 2, half, width), F32),
            vm((2, 2, kpad, width // 2), F32),
            vm((2, 2, width // 2, kpad), BF16),
            vm((2, 2, width // 2, kpad), BF16),
            vm((2, plane, width // 2, slots), F32),
            vm((2, plane, width // 2, slots), F32),
            vm((slots, width), F32),
            dma((plane,)),
            dma((plane + 1,)),
            dma((plane,)),
            dma((plane + 1,)),
            dma((nz,)),
            dma((nz,)),
            dma((nz,)),
            dma((nz,)),
            dma((nz,)),
            dma((2, nz)),
            dma((2, 2, nz)),
            dma((2, nz, 2)),
            dma((2, nz)),
            dma((2, plane)),
            dma((2, plane)),
        ],
        compiler_params=pltpu.CompilerParams(collective_id=0, has_side_effects=True),
        name="ewald_layer",
    )(cell_counts, neighbours, nbr_count, masked, pos8, kv8, filters, w_msg, w_val, w_one, w_two)


def solution(mesh):
    nz = 4 if mesh.shape["waves"] % 4 == 0 else 2
    placed = (
        P(("rows", "waves"), None),
        P(None, ("rows", "waves")),
        P(("rows", "waves")),
        P(("rows", "waves"), None),
        P(("rows", "waves")),
        P(None, "waves"),
        P("waves", None),
        P(),
        P(),
        P(),
        P(),
    )
    return jax.shard_map(
        functools.partial(shards, nz),
        mesh=mesh,
        in_specs=placed,
        out_specs=P(("rows", "waves"), None),
        check_vma=False,
    )
```

profile of v0, /device:TPU:0, one launch (start us, length us, event | category | flops | bytes accessed | tf_op | source)
XLA Modules:
  0.0 88.4 jit_solution(4633273972062271379)
XLA Ops:
  0.0 0.7 fusion
  0.7 0.7 broadcast_multiply_fusion.1
  1.4 0.0 copy-start
  1.4 0.6 pad.9.kv
  2.0 0.1 copy-done
  2.1 0.6 pad.8.pos
  2.7 1.8 %broadcast_multiply_fusion.feats = f32[256,256]{1,0:T(8,128)} fusion(f32[256,256]{1,0:T(8,128)} %param.11, f32[256]{0:T(256)S(1)} %fusion), kind=kLoop, calls=%fused_computation | loop fusion | flops 65536 | bytes 525312 | tf_op jit(solution)/shard_map/mul | solution.py:447
  4.5 82.2 %ewald_layer.1 = f32[256,256]{1,0:T(8,128)} custom-call(s32[2]{0:T(128)} %counts.1, s32[2,5]{1,0:T(2,128)} %neigh.1, s32[2]{0:T(128)} %ncount.1, f32[256,256]{1,0:T(8,128)} %broadcast_multiply_fusion.feats, f32[8,256]{1,0:T(8,128)} %pad.8.pos, f32[8,256]{1,0:T(8,128)} %pad.9.kv, f32[192,256]{1,0:T(8,128)} %filt.1, f32[256,256]{1,0:T(8,128)} %w_msg.1, ...), custom_call_target="tpu_custom_call" | custom-call | tf_op jit(solution)/shard_map/ewald_layer/pallas_call | solution.py:455
  86.7 1.7 %copy.13 = f32[256,256]{1,0:T(8,128)} copy(f32[256,256]{1,0:T(8,128)} %ewald_layer.1) | data formatting | bytes 524288
Async XLA Ops:
  1.4 0.7 copy-start
where the time goes:
time: 88.6 us; the launch traced here: 88.4 us
  Pallas kernels  82.2 us (93%)
  other arithmetic  3.17 us (4%)
  local copies, waits for them, and re-layouts  2.96 us (3%)
    pallas_call x1, Pallas kernels, shards(): pl.pallas_call(functools.partial(body, nz, plane, scale), out_shape=jax.S...  82.2 us

commit v1 on v0

v1 whole, which is shorter than its diff:
```python
import functools
import math

import jax
import jax.numpy as jnp
from jax import lax
from jax.experimental import pallas as pl
from jax.experimental.pallas import tpu as pltpu
from jax.sharding import PartitionSpec as P

MESH = pl.DeviceIdType.MESH
F32 = jnp.float32
BF16 = jnp.bfloat16

SIN = (4.44286798, -7.30744541, 3.5948021, -0.78440363)
COS = (1.4142135, -6.97885099, 5.73946117, -1.88356299, 0.31069819)


def split(x):
    high = x.astype(BF16)
    return high, (x - high.astype(F32)).astype(BF16)


def split3(x):
    a = x.astype(BF16).astype(F32)
    rest = x - a
    b = rest.astype(BF16).astype(F32)
    return a, b, rest - b


def mm(a, b):
    return jnp.dot(a, b, preferred_element_type=F32)


def dot3(a, b):
    return mm(a[0], b[0]) + mm(a[0], b[1]) + mm(a[1], b[0])


def horner(y, coefficients):
    total = y * coefficients[-1] + coefficients[-2]
    for coefficient in coefficients[-3::-1]:
        total = total * y + coefficient
    return total


def sincos(turns):
    x = turns - jnp.round(turns)
    y = x * x
    s = x * horner(y, SIN)
    c = horner(y, COS)
    return s * c, 1.0 - s * s


def columns(rows):
    height, width = rows.shape
    return jnp.concatenate([rows, jnp.zeros((128 - height, width), F32)], axis=0).T


def body(
    nz, plane, scale,
    counts, neigh, ncount, feats_in, pos_in, kv_in, filt_in, w_msg_in, w_val_in, w_one_in, w_two_in,
    out,
    feats, pos3, kv3, filt, w_msg, w_val, w_one, w_two,
    fm, pos, kv, vals, vals_all, pos_all, kv_all, near_feat, near_pos, km, ch, cl, sh, sl, fcat,
    s_acc, xbuf, zs, zr, f_all, fth, ftl, es, er, msg,
    s_in, s_pos, r_pos, s_val, r_val, s_near, r_near, s_kv, r_kv, s_x, r_x, s_z, r_z, s_f, r_f, s_g, s_e, r_e,
):
    slots, width = feats.shape
    kb = filt.shape[0]
    half = kb // 2
    hw = width // 2
    kall = nz * kb
    kpad = km.shape[0]
    cells = counts.shape[0]
    cell = slots // cells
    waves = nz * plane
    r = lax.axis_index("rows")
    w = lax.axis_index("waves")
    z = w // plane
    p = w % plane
    other = (1 - r, w)
    place = r * waves + w
    devices = 2 * waves
    scope = jax.named_scope

    def place_dev(q):
        return (q // waves, q % waves)

    prev_dev = place_dev((place + devices - 1) % devices)
    next_dev = place_dev((place + 1) % devices)

    def plane_dev(j):
        return (r, z * plane + (p + j) % plane)

    def z_dev(j):
        return (r, ((z + j) % nz) * plane + p)

    def rcopy(src, dst, ssem, rsem, dev):
        return pltpu.make_async_remote_copy(
            src_ref=src, dst_ref=dst, send_sem=ssem, recv_sem=rsem, device_id=dev, device_id_type=MESH
        )

    def rows_of(block):
        return pl.ds(pl.multiple_of(block * slots, slots), slots)

    loads = [
        pltpu.make_async_copy(src, dst, s_in.at[i])
        for i, (src, dst) in enumerate(
            (
                (pos_in, pos3),
                (kv_in, kv3),
                (feats_in, feats),
                (w_val_in, w_val),
                (filt_in, filt),
                (w_msg_in, w_msg),
                (w_one_in, w_one),
                (w_two_in, w_two),
            )
        )
    ]
    for load in loads:
        load.start()

    barrier = pltpu.get_barrier_semaphore()
    for dev in (other, prev_dev, next_dev):
        pl.semaphore_signal(barrier, inc=1, device_id=dev, device_id_type=MESH)
    for j in range(1, nz):
        pl.semaphore_signal(barrier, inc=1, device_id=z_dev(j), device_id_type=MESH)

    @pl.loop(1, plane)
    def _(j):
        pl.semaphore_signal(barrier, inc=1, device_id=plane_dev(j), device_id_type=MESH)

    with scope("A_load"):
        loads[0].wait()
        loads[1].wait()
        pos[...] = jnp.zeros_like(pos)
        pos[0:3, :] = pos3[...]
        kv[...] = jnp.zeros_like(kv)
        kv[0:3, 0:kb] = kv3[...] * (0.5 / math.pi)
        loads[2].wait()
        slot_ids = lax.broadcasted_iota(jnp.int32, (cell, width), 0)
        for c in range(cells):
            part = slice(c * cell, (c + 1) * cell)
            fm[part, :] = jnp.where(slot_ids < counts[c], feats[part, :], 0.0)
        loads[3].wait()
        projected = dot3(split(fm[...]), split(w_val[...]))
        for h in range(2):
            vals[h] = projected[:, h * hw : (h + 1) * hw]

    with scope("A_barrier"):
        pl.semaphore_wait(barrier, nz + plane + 1)

    def kv_copy(j):
        return rcopy(kv, kv_all.at[z], s_kv.at[j], r_kv.at[z], z_dev(j))

    def kv_arrival(j):
        q = (z + j) % nz
        return rcopy(kv, kv_all.at[q], s_kv.at[j], r_kv.at[q], z_dev(j))

    def pos_copy(j):
        return rcopy(pos, pos_all.at[p], s_pos.at[j], r_pos.at[p], plane_dev(j))

    def pos_arrival(q):
        return rcopy(pos, pos_all.at[q], s_pos.at[0], r_pos.at[q], other)

    def val_copy(h, j):
        return rcopy(vals.at[h], vals_all.at[h, p], s_val.at[h, j], r_val.at[h, p], plane_dev(j))

    def val_arrival(h, q):
        return rcopy(vals.at[h], vals_all.at[h, q], s_val.at[h, 0], r_val.at[h, q], other)

    def near_copies(side):
        dev = next_dev if side == 0 else prev_dev
        return (
            rcopy(pos, near_pos.at[side], s_near.at[side, 0], r_near.at[side, 0], dev),
            rcopy(fm, near_feat.at[side], s_near.at[side, 1], r_near.at[side, 1], dev),
        )

    for j in range(1, nz):
        kv_copy(j).start()

    @pl.loop(1, plane)
    def _(j):
        pos_copy(j).start()

    for h in range(2):

        @pl.loop(1, plane)
        def _(j):
            val_copy(h, j).start()

    for side in range(2):
        for copy in near_copies(side):
            copy.start()

    def place_k(block, rows):
        a, b, c = split3(rows)
        stack = [a, a, a, b, b, b, c, c, c]
        stack.append(jnp.zeros((128 - 8 * len(stack), rows.shape[1]), F32))
        km[pl.ds(pl.multiple_of(block * kb, 16), kb), :] = jnp.concatenate(stack, axis=0).T[:kb].astype(BF16)

    def place_v(h, q, block):
        a, b = split(block)
        fcat[h, rows_of(q), 0:hw] = a
        fcat[h, rows_of(q), hw:width] = b

    if kpad > kall:
        f_all[:, :, kall:, :] = jnp.zeros((2, 2, kpad - kall, hw), F32)
    for h in range(2):
        place_v(h, p, vals[h])
    with scope("B_kv"):
        place_k(z, kv[...])
        if kpad > kall:
            km[kall:, :] = jnp.zeros((kpad - kall, 128), BF16)
        for j in range(1, nz):
            kv_arrival(j).wait_recv()
            q = (z + j) % nz
            place_k(q, kv_all[q])

    def phases(q, rows3):
        stack = list(split3(rows3)) * 3
        stack.append(jnp.zeros((128 - 8 * len(stack), slots), F32))
        s, c = sincos(mm(km[...], jnp.concatenate(stack, axis=0).astype(BF16)))
        lanes = rows_of(q)
        a, b = split(c)
        ch[:, lanes] = a
        cl[:, lanes] = b
        a, b = split(s)
        sh[:, lanes] = a
        sl[:, lanes] = b

    pos_all[p] = pos[...]

    with scope("C_phases"):

        @pl.loop(0, plane)
        def _(j):
            q = (p + j) % plane

            @pl.when(j > 0)
            def _():
                pos_arrival(q).wait_recv()

            phases(q, pos_all[q])

    natoms = plane * slots
    lower = z < nz // 2
    rank = jnp.where(lower, z, nz - 1 - z)
    ahead = jnp.where(lower, 0, 1)
    inner = rank > 0

    def block_at(j):
        far = nz - 1 - rank
        block = jnp.where(j < far, nz - 1 - j, j - far)
        return jnp.where(lower, block, nz - 1 - block)

    def partial_sums(h, j):
        zb = block_at(j)
        ks = pl.ds(pl.multiple_of(zb * kb, 16), kb)
        for part, (hi, lo) in enumerate(((ch, cl), (sh, sl))):
            wide = mm(hi[ks, :], fcat[h])
            total = wide[:, :hw] + wide[:, hw:] + mm(lo[ks, :], fcat[h, :, 0:hw])
            for c in range(2):
                s_acc[h, zb, c, part] = total[c * half : (c + 1) * half]

    def x_copy(h, j):
        zb = block_at(j)
        return rcopy(s_acc.at[h, zb, 1 - r], xbuf.at[h, zb], s_x.at[h, zb], r_x.at[h, zb], other)

    def step(way):
        return (r, (z + 1 - 2 * way) * plane + p)

    def s_hop(h, zb, part, way):
        return rcopy(
            zs.at[h, zb, part], zr.at[way, h, zb, part], s_z.at[h, zb, part], r_z.at[way, h, zb, part], step(way)
        )

    def add_arrival(h, zb, part, way):
        s_hop(h, zb, part, way).wait_recv()
        zs[h, zb, part] = zs[h, zb, part] + zr[way, h, zb, part]

    def pass_on(h, j):
        zb = block_at(j)
        x_copy(h, j).wait_recv()
        forward = j < nz - 1 - rank
        for part in range(2):
            zs[h, zb, part] = s_acc[h, zb, r, part] + xbuf[h, zb, part]
        for part in range(2):

            @pl.when(inner & (forward | (j == nz - 1)))
            def _():
                add_arrival(h, zb, part, ahead)

            @pl.when(jnp.logical_not(forward))
            def _():
                add_arrival(h, zb, part, 1 - ahead)

            if j < nz - 1:
                s_hop(h, zb, part, jnp.where(forward, ahead, 1 - ahead)).start()

    def share(h, part, zb, c):
        return f_all.at[h, part, pl.ds(pl.multiple_of((zb * 2 + c) * half, 8), half), :]

    def f_hop(h, part, zb, way, d):
        here = share(h, part, zb, r)
        return rcopy(here, here, s_f.at[h, part, way, d], r_f.at[h, part, zb, r], step(way))

    def f_relay(h, part, zb):
        here = share(h, part, zb, r)
        return rcopy(here, here, s_g.at[h, part, zb], r_f.at[h, part, zb, r], other)

    def f_arrival(h, part, zb, c):
        here = share(h, part, zb, c)
        return rcopy(here, here, s_g.at[h, part, zb], r_f.at[h, part, zb, c], other)

    mine = pl.multiple_of(r * half, 8)

    def f_own(h):
        own_filter = filt[pl.ds(mine, half), h * hw : (h + 1) * hw] * scale
        for part in range(2):
            f_all[h, part, pl.ds(pl.multiple_of((z * 2 + r) * half, 8), half), :] = own_filter * zs[h, z, part]
            for way, more in ((0, z < nz - 1), (1, z > 0)):

                @pl.when(more)
                def _():
                    f_hop(h, part, z, way, 0).start()

            f_relay(h, part, z).start()

    def f_pass(h, d):
        for part in range(2):
            for way, there, more in ((0, z >= d, z < nz - 1), (1, z + d < nz, z > 0)):
                zb = z - d if way == 0 else z + d

                @pl.when(there)
                def _():
                    f_arrival(h, part, zb, r).wait_recv()

                @pl.when(there & more)
                def _():
                    f_hop(h, part, zb, way, d).start()

                @pl.when(there)
                def _():
                    f_relay(h, part, zb).start()

    def back(h, q):
        lanes = rows_of(q)
        return dot3((fth[h, 0], ftl[h, 0]), (ch[:, lanes], cl[:, lanes])) + dot3(
            (fth[h, 1], ftl[h, 1]), (sh[:, lanes], sl[:, lanes])
        )

    def e_copy(h, j):
        return rcopy(es.at[h, j], er.at[h, j], s_e.at[h, j], r_e.at[h, j], plane_dev(j))

    def gather_half(h):
        for part in range(2):
            for zb in range(nz):
                f_arrival(h, part, zb, 1 - r).wait_recv()
            a, b = split(f_all[h, part].T)
            fth[h, part] = a
            ftl[h, part] = b

    def back_range(h, start, stop):
        @pl.loop(start, stop)
        def _(j):
            es[h, j] = back(h, (p + j) % plane)
            e_copy(h, j).start()

    def take_vals(h):
        @pl.loop(1, plane)
        def _(j):
            q = (p + j) % plane
            val_arrival(h, q).wait_recv()
            place_v(h, q, vals_all[h, q])

    def own_message():
        first = place * cells
        total_cells = cells * devices
        own_cols = columns(pos[...])
        same = lax.broadcasted_iota(jnp.int32, (slots, slots), 0) == lax.broadcasted_iota(
            jnp.int32, (slots, slots), 1
        )
        row_cell = lax.broadcasted_iota(jnp.int32, (slots, slots), 0) // cell
        col_cell = lax.broadcasted_iota(jnp.int32, (slots, slots), 1) // cell

        def listed(c, target):
            found = jnp.float32(0.0)
            for b in range(neigh.shape[1]):
                hit = (neigh[c, b] == target) & (b < ncount[c])
                found = found + jnp.where(hit, 1.0, 0.0)
            return found

        gathered = jnp.zeros((slots, width), F32)
        for shift in (-1, 0, 1):
            if shift:
                for copy in near_copies(0 if shift < 0 else 1):
                    copy.wait_recv()
            near = pos[...] if shift == 0 else near_pos[0 if shift < 0 else 1]
            atoms = fm[...] if shift == 0 else near_feat[0 if shift < 0 else 1]
            dist = jnp.zeros((slots, slots), F32)
            for axis in range(3):
                diff = own_cols[:, axis : axis + 1] - near[axis : axis + 1]
                dist = dist + diff * diff
            live = jnp.zeros((slots, slots), F32)
            for c in range(cells):
                for t in range(cells):
                    target = (first + shift * cells + t + total_cells) % total_cells
                    live = jnp.where((row_cell == c) & (col_cell == t), listed(c, target), live)
            weight = jnp.exp(-0.125 * dist) * live
            if shift == 0:
                weight = jnp.where(same, 0.0, weight)
            gathered = gathered + dot3(split(weight), split(atoms))
        msg[...] = feats[...] + 0.125 * dot3(split(gathered), split(w_msg[...]))

    with scope("D_takeA"):
        take_vals(0)
    with scope("D_psumA"):
        for j in range(nz):
            partial_sums(0, j)
            x_copy(0, j).start()
            if j:

                @pl.when(jnp.logical_not(inner))
                def _():
                    pass_on(0, j - 1)

    with scope("D_passA01"):

        @pl.when(inner)
        def _():
            for j in range(nz // 2):
                pass_on(0, j)

    with scope("E_takeB"):
        take_vals(1)
    with scope("E_psumB"):
        for j in range(nz):
            partial_sums(1, j)
            x_copy(1, j).start()
            if j:

                @pl.when(jnp.logical_not(inner))
                def _():
                    pass_on(1, j - 1)

    with scope("E_passA2"):

        @pl.when(inner)
        def _():
            for j in range(nz // 2, nz - 1):
                pass_on(0, j)

    for load in loads[4:]:
        load.wait()
    with scope("F_passA3"):
        pass_on(0, nz - 1)
    with scope("F_ownA"):
        f_own(0)
    with scope("F_msg"):
        own_message()
    with scope("G_passB01"):

        @pl.when(inner)
        def _():
            for j in range(nz // 2):
                pass_on(1, j)

    with scope("G_fpassA1"):
        f_pass(0, 1)
    with scope("G_passB2"):

        @pl.when(inner)
        def _():
            for j in range(nz // 2, nz - 1):
                pass_on(1, j)

    with scope("G_fpassA2e"):

        @pl.when(jnp.logical_not(inner))
        def _():
            for d in range(2, nz - 1):
                f_pass(0, d)

    with scope("H_passB3"):
        pass_on(1, nz - 1)
    with scope("H_ownB"):
        f_own(1)
    with scope("H_fpassA2i"):

        @pl.when(inner)
        def _():
            for d in range(2, nz - 1):
                f_pass(0, d)

        if nz > 2:
            f_pass(0, nz - 1)
    with scope("I_gatherA"):
        gather_half(0)
    with scope("I_backA"):
        back_range(0, 1, plane)
    with scope("J_fpassB"):
        for d in range(1, nz):
            f_pass(1, d)
    with scope("K_gatherB"):
        gather_half(1)
    with scope("K_backB"):
        back_range(1, 1, plane)
    with scope("L_own"):
        for h in range(2):
            es[h, 0] = back(h, p)

    with scope("M_ewait"):
        for h in range(2):

            @pl.loop(1, plane)
            def _(j):
                e_copy(h, j).wait_recv()
                es[h, 0] = es[h, 0] + er[h, j]

    with scope("N_mlp"):
        summed = msg[...] + jnp.concatenate([es[0, 0].T, es[1, 0].T], axis=1)
        normed = summed / jnp.sqrt(jnp.mean(summed * summed, axis=1, keepdims=True) + 1e-06)
        v = dot3(split(normed), split(w_one[...]))
        hidden = v / (1.0 + jnp.exp(-v))
        result = summed + dot3(split(hidden), split(w_two[...]))
        for c in range(cells):
            part = slice(c * cell, (c + 1) * cell)
            out[part, :] = jnp.where(slot_ids < counts[c], result[part], 0.0)

    for j in range(1, nz):
        kv_copy(j).wait_send()
    for h in range(2):
        for j in range(nz):
            x_copy(h, j).wait_send()
            if j < nz - 1:
                for part in range(2):
                    s_hop(h, block_at(j), part, 0).wait_send()
        for part in range(2):
            for zb in range(nz):
                f_relay(h, part, zb).wait_send()
            for d in range(nz):
                for way, there, more in ((0, z >= d, z < nz - 1), (1, z + d < nz, z > 0)):

                    @pl.when(there & more)
                    def _():
                        f_hop(h, part, z - d if way == 0 else z + d, way, d).wait_send()

    @pl.loop(1, plane)
    def _(j):
        pos_copy(j).wait_send()
        for h in range(2):
            val_copy(h, j).wait_send()
            e_copy(h, j).wait_send()

    for side in range(2):
        for copy in near_copies(side):
            copy.wait_send()


def shards(
    nz, feats, positions, cell_counts, neighbours, nbr_count, kvec, filters, w_msg, w_val, w_one, w_two
):
    slots, width = feats.shape
    kb = kvec.shape[1]
    waves = lax.axis_size("waves")
    plane = waves // nz
    devices = lax.axis_size("rows") * waves
    kpad = -(-nz * kb // 128) * 128
    kbpad = -(-kb // 128) * 128
    half = kb // 2
    hw = width // 2
    scale = 1.0 / math.sqrt(float(slots * devices) * float(kb * waves))
    natoms = plane * slots
    vm = pltpu.VMEM
    dma = pltpu.SemaphoreType.DMA
    smem_spec = pl.BlockSpec(memory_space=pltpu.SMEM)
    any_spec = pl.BlockSpec(memory_space=pl.ANY)
    vmem_spec = pl.BlockSpec(memory_space=pltpu.VMEM)
    return pl.pallas_call(
        functools.partial(body, nz, plane, scale),
        out_shape=jax.ShapeDtypeStruct((slots, width), F32),
        in_specs=[smem_spec] * 3 + [any_spec] * 8,
        out_specs=vmem_spec,
        scratch_shapes=[
            vm((slots, width), F32),
            vm((3, slots), F32),
            vm((3, kb), F32),
            vm((kb, width), F32),
            vm((width, width), F32),
            vm((width, width), F32),
            vm((width, width), F32),
            vm((width, width), F32),
            vm((slots, width), F32),
            vm((8, slots), F32),
            vm((8, kbpad), F32),
            vm((2, slots, hw), F32),
            vm((2, plane, slots, hw), F32),
            vm((plane, 8, slots), F32),
            vm((nz, 8, kbpad), F32),
            vm((2, slots, width), F32),
            vm((2, 8, slots), F32),
            vm((kpad, 128), BF16),
            vm((kpad, natoms), BF16),
            vm((kpad, natoms), BF16),
            vm((kpad, natoms), BF16),
            vm((kpad, natoms), BF16),
            vm((2, natoms, width), BF16),
            vm((2, nz, 2, 2, half, hw), F32),
            vm((2, nz, 2, half, hw), F32),
            vm((2, nz, 2, half, hw), F32),
            vm((2, 2, nz, 2, half, hw), F32),
            vm((2, 2, kpad, hw), F32),
            vm((2, 2, hw, kpad), BF16),
            vm((2, 2, hw, kpad), BF16),
            vm((2, plane, hw, slots), F32),
            vm((2, plane, hw, slots), F32),
            vm((slots, width), F32),
            dma((8,)),
            dma((plane,)),
            dma((plane,)),
            dma((2, plane)),
            dma((2, plane)),
            dma((2, 2)),
            dma((2, 2)),
            dma((nz,)),
            dma((nz,)),
            dma((2, nz)),
            dma((2, nz)),
            dma((2, nz, 2)),
            dma((2, 2, nz, 2)),
            dma((2, 2, 2, nz)),
            dma((2, 2, nz, 2)),
            dma((2, 2, nz)),
            dma((2, plane)),
            dma((2, plane)),
        ],
        compiler_params=pltpu.CompilerParams(collective_id=0, has_side_effects=True),
        name="ewald_layer",
    )(cell_counts, neighbours, nbr_count, feats, positions, kvec, filters, w_msg, w_val, w_one, w_two)


def solution(mesh):
    nz = 4 if mesh.shape["waves"] % 4 == 0 else 2
    placed = (
        P(("rows", "waves"), None),
        P(None, ("rows", "waves")),
        P(("rows", "waves")),
        P(("rows", "waves"), None),
        P(("rows", "waves")),
        P(None, "waves"),
        P("waves", None),
        P(),
        P(),
        P(),
        P(),
    )
    return jax.shard_map(
        functools.partial(shards, nz),
        mesh=mesh,
        in_specs=placed,
        out_specs=P(("rows", "waves"), None),
        check_vma=False,
    )
```

time: 88.6 us -> 69.1 us (0.78)
  Pallas kernels: 82.2 us -> 67.3 us
  other arithmetic: 3.17 us -> 0 us
  local copies, waits for them, and re-layouts: 2.96 us -> 1.67 us
    pallas_call x1, Pallas kernels: 82.2 us -> 67.3 us  [shards(): pl.pallas_call(functools.partial(body, nz, plane, scale), out_shape=jax.S...]
    mul x2 -> x0, other arithmetic: 2.44 us -> none  [the longest x1 1.75 us: shards(): masked = feats * valid[:, None]]
    pad x2 -> x0, local copies, waits for them, and re-layouts: 1.21 us -> none  [the longest x1 0.61 us: shards(): kv8 = jnp.pad(kvec * (0.5 / math.pi), ((0, 5), (0, kbpad - kb)))]
where the time goes in v1:
time: 69.1 us; the launch traced here: 68.9 us
  Pallas kernels  67.3 us (97%)
  local copies, waits for them, and re-layouts  1.67 us (2%)
    pallas_call x1, Pallas kernels, shards(): pl.pallas_call(functools.partial(body, nz, plane, scale), out_shape=jax.S...  67.3 us
    unnamed x1, local copies, waits for them, and re-layouts  1.67 us

profile of v1, /device:TPU:0, one launch (start us, length us, event | category | flops | bytes accessed | tf_op | source)
XLA Modules:
  0.0 68.9 jit_solution(17233414646837396640)
XLA Ops:
  0.0 67.3 %ewald_layer.1 = f32[256,256]{1,0:T(8,128)} custom-call(s32[2]{0:T(128)} %counts.1, s32[2,5]{1,0:T(2,128)} %neigh.1, s32[2]{0:T(128)} %ncount.1, f32[256,256]{1,0:T(8,128)} %feats_in.1, f32[3,256]{1,0:T(4,128)} %pos_in.1, f32[3,192]{1,0:T(4,128)} %kv_in.1, f32[192,256]{1,0:T(8,128)} %filt_in.1, f32[256,256]{1,0:T(8,128)} %w_msg_in.1, f32[256,256]{1,0:T(8,128)} %w_val_in.1, ...), custom_call_target="tpu_custom_call" | custom-call | tf_op jit(solution)/shard_map/ewald_layer/pallas_call | solution.py:581
  67.3 1.7 %copy.13 = f32[256,256]{1,0:T(8,128)} copy(f32[256,256]{1,0:T(8,128)} %ewald_layer.1) | data formatting | bytes 524288

commit v2 on v1

v2 whole, which is shorter than its diff:
```python
import functools
import math

import jax
import jax.numpy as jnp
from jax import lax
from jax.experimental import pallas as pl
from jax.experimental.pallas import tpu as pltpu
from jax.sharding import PartitionSpec as P

MESH = pl.DeviceIdType.MESH
F32 = jnp.float32
BF16 = jnp.bfloat16

SIN = (4.44286798, -7.30744541, 3.5948021, -0.78440363)
COS = (1.4142135, -6.97885099, 5.73946117, -1.88356299, 0.31069819)


def split(x):
    high = x.astype(BF16)
    return high, (x - high.astype(F32)).astype(BF16)


def split3(x):
    a = x.astype(BF16).astype(F32)
    rest = x - a
    b = rest.astype(BF16).astype(F32)
    return a, b, rest - b


def mm(a, b):
    return jnp.dot(a, b, preferred_element_type=F32)


def dot3(a, b):
    return mm(a[0], b[0]) + mm(a[0], b[1]) + mm(a[1], b[0])


def horner(y, coefficients):
    total = y * coefficients[-1] + coefficients[-2]
    for coefficient in coefficients[-3::-1]:
        total = total * y + coefficient
    return total


def sincos(turns):
    x = turns - jnp.round(turns)
    y = x * x
    s = x * horner(y, SIN)
    c = horner(y, COS)
    return s * c, 1.0 - s * s


def columns(rows):
    height, width = rows.shape
    return jnp.concatenate([rows, jnp.zeros((128 - height, width), F32)], axis=0).T


def body(
    nz, plane, scale,
    counts_in, neigh_in, ncount_in, feats_in, pos_in, kv_in, filt_in, w_msg_in, w_val_in, w_one_in, w_two_in,
    out,
    counts, neigh, ncount, feats, pos3, kv3, filt, w_msg, w_val, w_one, w_two,
    fm, pos, kv, vals, vals_all, pos_all, kv_all, near_feat, near_pos, via_feat, via_pos, km, ch, cl, sh, sl, fcat,
    s_acc, xbuf, zs, zr, f_all, ft, es, er, msg, filt_far,
    s_in, s_pos, r_pos, s_val, r_val, s_near, r_near, s_via, r_via, s_on, s_kv, r_kv, s_x, r_x, s_z, r_z, s_f, r_f, s_g, s_e, r_e, s_filt, r_filt,
):
    slots, width = feats.shape
    kb = filt.shape[0]
    half = kb // 2
    hw = width // 2
    qw = hw // 2
    pieces = 4
    kall = nz * kb
    kpad = km.shape[0]
    cells = counts.shape[0]
    cell = slots // cells
    waves = nz * plane
    r = lax.axis_index("rows")
    w = lax.axis_index("waves")
    z = w // plane
    p = w % plane
    other = (1 - r, w)
    place = r * waves + w
    devices = 2 * waves
    scope = jax.named_scope
    at_low = p == 0
    at_high = p == plane - 1
    at_edge = at_low | at_high
    facing = z * plane + plane - 1 - p
    met = at_edge & ((z == 0) | (z == nz - 1))

    def plane_dev(j):
        return (r, z * plane + (p + j) % plane)

    def z_dev(j):
        return (r, ((z + j) % nz) * plane + p)

    def rcopy(src, dst, ssem, rsem, dev):
        return pltpu.make_async_remote_copy(
            src_ref=src, dst_ref=dst, send_sem=ssem, recv_sem=rsem, device_id=dev, device_id_type=MESH
        )

    def rows_of(block):
        return pl.ds(pl.multiple_of(block * slots, slots), slots)

    loads = [
        pltpu.make_async_copy(src, dst, s_in.at[i])
        for i, (src, dst) in enumerate(
            (
                (pos_in, pos3),
                (kv_in, kv3),
                (feats_in, feats),
                (w_val_in, w_val),
                (filt_in, filt),
                (w_msg_in, w_msg),
                (w_one_in, w_one),
                (w_two_in, w_two),
                (counts_in, counts),
                (neigh_in, neigh),
                (ncount_in, ncount),
            )
        )
    ]
    for load in loads:
        load.start()

    natoms = plane * slots
    lower = z < nz // 2
    rank = jnp.where(lower, z, nz - 1 - z)
    side_z = nz // 2
    inner = rank == side_z - 1
    outer = jnp.logical_not(inner)
    sign = jnp.where(lower, 1, -1)
    toward = (r, (z + sign) * plane + p)
    away = (r, (z - sign) * plane + p)

    def block_at(j):
        block = nz - 1 - j if j < side_z else j - side_z
        return jnp.where(lower, block, nz - 1 - block)

    mine = pl.multiple_of(r * half, 8)

    barrier = pltpu.get_barrier_semaphore()
    pl.semaphore_signal(barrier, inc=1, device_id=other, device_id_type=MESH)

    @pl.when(met)
    def _():
        pl.semaphore_signal(barrier, inc=1, device_id=(1 - r, facing), device_id_type=MESH)

    for j in range(1, nz):
        pl.semaphore_signal(barrier, inc=1, device_id=z_dev(j), device_id_type=MESH)

    @pl.loop(1, plane)
    def _(j):
        pl.semaphore_signal(barrier, inc=1, device_id=plane_dev(j), device_id_type=MESH)

    with scope("A_load"):
        loads[0].wait()
        loads[1].wait()
        pos[...] = jnp.zeros_like(pos)
        pos[0:3, :] = pos3[...]
        kv[...] = jnp.zeros_like(kv)
        kv[0:3, 0:kb] = kv3[...] * (0.5 / math.pi)
        loads[2].wait()
        for load in loads[8:]:
            load.wait()
        slot_ids = lax.broadcasted_iota(jnp.int32, (cell, width), 0)
        for c in range(cells):
            part = slice(c * cell, (c + 1) * cell)
            fm[part, :] = jnp.where(slot_ids < counts[c], feats[part, :], 0.0)
        loads[3].wait()
        projected = dot3(split(fm[...]), split(w_val[...]))
        for h in range(2):
            vals[h] = projected[:, h * hw : (h + 1) * hw]

    loads[4].wait()
    with scope("A_barrier"):
        pl.semaphore_wait(barrier, nz + plane - 1 + jnp.where(met, 1, 0))

    def kv_copy(j):
        return rcopy(kv, kv_all.at[z], s_kv.at[j], r_kv.at[z], z_dev(j))

    def kv_arrival(j):
        q = (z + j) % nz
        return rcopy(kv, kv_all.at[q], s_kv.at[j], r_kv.at[q], z_dev(j))

    def pos_copy(j):
        return rcopy(pos, pos_all.at[p], s_pos.at[j], r_pos.at[p], plane_dev(j))

    def pos_arrival(q):
        return rcopy(pos, pos_all.at[q], s_pos.at[0], r_pos.at[q], other)

    def val_copy(h, j):
        return rcopy(vals.at[h], vals_all.at[h, p], s_val.at[h, j], r_val.at[h, p], plane_dev(j))

    def val_arrival(h, q):
        return rcopy(vals.at[h], vals_all.at[h, q], s_val.at[h, 0], r_val.at[h, q], other)

    def pair(feat_src, pos_src, feat_dst, pos_dst, ssem, rsem, dev):
        return (
            rcopy(pos_src, pos_dst, ssem.at[0], rsem.at[0], dev),
            rcopy(feat_src, feat_dst, ssem.at[1], rsem.at[1], dev),
        )

    def near_copies(side):
        dev = plane_dev(1 if side == 0 else plane - 1)
        return pair(fm, pos, near_feat.at[side], near_pos.at[side], s_near.at[side], r_near.at[side], dev)

    def via_copies():
        dev = (r, ((z + jnp.where(at_high, 1, nz - 1)) % nz) * plane + p)
        return pair(fm, pos, via_feat, via_pos, s_via, r_via, dev)

    def on_copies():
        side = jnp.where(at_high, 0, 1)
        flip = (at_high & (z == 0)) | (at_low & (z == nz - 1))
        dev = (jnp.where(flip, 1 - r, r), facing)
        return pair(via_feat, via_pos, near_feat.at[side], near_pos.at[side], s_on, r_near.at[side], dev)

    def start_near():
        for side, there in ((0, jnp.logical_not(at_high)), (1, jnp.logical_not(at_low))):

            @pl.when(there)
            def _():
                for copy in near_copies(side):
                    copy.start()

        @pl.when(at_edge)
        def _():
            for arrived, copy in zip(via_copies(), on_copies()):
                arrived.wait_recv()
                copy.start()

    def filt_copy():
        return rcopy(filt.at[pl.ds(mine, half), :], filt_far, s_filt.at[0], r_filt.at[0], toward)

    for j in range(1, nz):
        kv_copy(j).start()

    if nz > 2:

        @pl.when(outer)
        def _():
            filt_copy().start()

    @pl.loop(1, plane)
    def _(j):
        pos_copy(j).start()

    @pl.loop(1, plane)
    def _(j):
        val_copy(0, j).start()

    def place_k(block, rows):
        a, b, c = split3(rows)
        stack = [a, a, a, b, b, b, c, c, c]
        stack.append(jnp.zeros((128 - 8 * len(stack), rows.shape[1]), F32))
        km[pl.ds(pl.multiple_of(block * kb, 16), kb), :] = jnp.concatenate(stack, axis=0).T[:kb].astype(BF16)

    def place_v(h, q, block):
        a, b = split(block)
        fcat[h, rows_of(q), 0:hw] = a
        fcat[h, rows_of(q), hw:width] = b

    if kpad > kall:
        f_all[:, kall:, :] = jnp.zeros((pieces, kpad - kall, hw), F32)
    for h in range(2):
        place_v(h, p, vals[h])
    with scope("B_kv"):
        place_k(z, kv[...])
        if kpad > kall:
            km[kall:, :] = jnp.zeros((kpad - kall, 128), BF16)
        for j in [1, nz - 1] + list(range(2, nz - 1)) if nz > 2 else [1]:
            kv_arrival(j).wait_recv()
            if j == nz - 1:

                @pl.when(at_edge)
                def _():
                    for copy in via_copies():
                        copy.start()

            q = (z + j) % nz
            place_k(q, kv_all[q])

    def phases(q, rows3):
        stack = list(split3(rows3)) * 3
        stack.append(jnp.zeros((128 - 8 * len(stack), slots), F32))
        s, c = sincos(mm(km[...], jnp.concatenate(stack, axis=0).astype(BF16)))
        lanes = rows_of(q)
        a, b = split(c)
        ch[:, lanes] = a
        cl[:, lanes] = b
        a, b = split(s)
        sh[:, lanes] = a
        sl[:, lanes] = b

    pos_all[p] = pos[...]

    with scope("C_phases"):

        @pl.loop(0, plane)
        def _(j):
            q = (p + j) % plane

            @pl.when(j > 0)
            def _():
                with scope("c_poswait"):
                    pos_arrival(q).wait_recv()

            with scope("c_phase"):
                phases(q, pos_all[q])

            @pl.when(j == plane // 2)
            def _():
                @pl.loop(1, plane)
                def _(k):
                    val_copy(0, k).wait_send()

                @pl.loop(1, plane)
                def _(k):
                    val_copy(1, k).start()

    def partial_sums(h, j):
        zb = block_at(j)
        ks = pl.ds(pl.multiple_of(zb * kb, 16), kb)
        totals = []
        for hi, lo in ((ch, cl), (sh, sl)):
            wide = mm(hi[ks, :], fcat[h])
            totals.append(wide[:, :hw] + wide[:, hw:] + mm(lo[ks, :], fcat[h, :, 0:hw]))
        for i in range(2):
            piece = jnp.concatenate([total[:, i * qw : (i + 1) * qw] for total in totals], axis=1)
            for c in range(2):
                s_acc[h, zb, c, i] = piece[c * half : (c + 1) * half]

    def x_copy(h, j):
        zb = block_at(j)
        return rcopy(s_acc.at[h, zb, 1 - r], xbuf.at[h, zb], s_x.at[h, zb], r_x.at[h, zb], other)

    def s_hop(u, j, source):
        zb = block_at(j)
        return rcopy(zs.at[u, zb], zr.at[source, u, zb], s_z.at[u, zb], r_z.at[source, u, zb], toward)

    def gathered_sum(u, j, sources):
        zb = block_at(j)
        if u % 2 == 0:
            x_copy(u // 2, j).wait_recv()
        total = s_acc[u // 2, zb, r, u % 2] + xbuf[u // 2, zb, u % 2]
        for source in sources:
            s_hop(u, j, source).wait_recv()
            total = total + zr[source, u, zb]
        return total

    def send_sum(u, j, is_inner):
        zs[u, block_at(j)] = gathered_sum(u, j, (0,) if is_inner and nz > 2 else ())
        s_hop(u, j, 1 if is_inner else 0).start()

    def share(u, zb, c):
        return f_all.at[u, pl.ds(pl.multiple_of((zb * 2 + c) * half, 8), half), :]

    def f_hop(u, zb, way, dev):
        here = share(u, zb, r)
        return rcopy(here, here, s_f.at[u, zb, way], r_f.at[u, zb, r], dev)

    def f_relay(u, zb):
        here = share(u, zb, r)
        return rcopy(here, here, s_g.at[u, zb], r_f.at[u, zb, r], other)

    def f_arrival(u, zb, c):
        here = share(u, zb, c)
        return rcopy(here, here, s_g.at[u, zb], r_f.at[u, zb, c], other)

    def finish_sum(u, j):
        zb = block_at(j)
        lanes = slice(u * qw, (u + 1) * qw)
        rows = filt[pl.ds(mine, half), lanes] if j == nz - 1 else filt_far[:, lanes]
        rows = jnp.concatenate([rows, rows], axis=1) * scale
        total = gathered_sum(u, j, (0, 1) if nz > 2 else (1,))
        f_all[u, pl.ds(pl.multiple_of((zb * 2 + r) * half, 8), half), :] = rows * total
        if nz > 2:
            f_hop(u, zb, 1, away).start()
        f_hop(u, zb, 0, toward).start()
        f_relay(u, zb).start()

    def take_filtered(u, j, is_inner):
        zb = block_at(j)
        f_arrival(u, zb, r).wait_recv()
        if is_inner and nz > 2:
            f_hop(u, zb, 1, away).start()
        f_relay(u, zb).start()

    def back(u, j):
        lanes = rows_of((p + j) % plane)
        total = jnp.zeros((qw, slots), F32)
        for part, (hi, lo) in enumerate(((ch, cl), (sh, sl))):
            both = mm(ft[u, part], hi[:, lanes])
            total = total + both[:qw] + both[qw:] + mm(ft[u, part, 0:qw, :], lo[:, lanes])
        es[u, j] = total

    def e_copy(u, j):
        return rcopy(es.at[u, j], er.at[u, j], s_e.at[u, j], r_e.at[u, j], plane_dev(j))

    def gather(u):
        for zb in range(nz):
            f_arrival(u, zb, 1 - r).wait_recv()
        a, b = split(f_all[u].T)
        for part in range(2):
            rows = slice(part * qw, (part + 1) * qw)
            ft[u, part, 0:qw, :] = a[rows]
            ft[u, part, qw:hw, :] = b[rows]

    def back_range(u, start, stop):
        @pl.loop(start, stop)
        def _(j):
            back(u, j)
            e_copy(u, j).start()

    def take_vals(h):
        @pl.loop(1, plane)
        def _(j):
            q = (p + j) % plane
            val_arrival(h, q).wait_recv()
            place_v(h, q, vals_all[h, q])

    def own_message():
        first = place * cells
        total_cells = cells * devices
        own_cols = columns(pos[...])
        same = lax.broadcasted_iota(jnp.int32, (slots, slots), 0) == lax.broadcasted_iota(
            jnp.int32, (slots, slots), 1
        )
        row_cell = lax.broadcasted_iota(jnp.int32, (slots, slots), 0) // cell
        col_cell = lax.broadcasted_iota(jnp.int32, (slots, slots), 1) // cell

        def listed(c, target):
            found = jnp.float32(0.0)
            for b in range(neigh.shape[1]):
                hit = (neigh[c, b] == target) & (b < ncount[c])
                found = found + jnp.where(hit, 1.0, 0.0)
            return found

        gathered = jnp.zeros((slots, width), F32)
        for shift in (-1, 0, 1):
            if shift:
                for copy in near_copies(0 if shift < 0 else 1):
                    copy.wait_recv()
            near = pos[...] if shift == 0 else near_pos[0 if shift < 0 else 1]
            atoms = fm[...] if shift == 0 else near_feat[0 if shift < 0 else 1]
            dist = jnp.zeros((slots, slots), F32)
            for axis in range(3):
                diff = own_cols[:, axis : axis + 1] - near[axis : axis + 1]
                dist = dist + diff * diff
            live = jnp.zeros((slots, slots), F32)
            for c in range(cells):
                for t in range(cells):
                    target = (first + shift * cells + t + total_cells) % total_cells
                    live = jnp.where((row_cell == c) & (col_cell == t), listed(c, target), live)
            weight = jnp.exp(-0.125 * dist) * live
            if shift == 0:
                weight = jnp.where(same, 0.0, weight)
            gathered = gathered + dot3(split(weight), split(atoms))
        msg[...] = feats[...] + 0.125 * dot3(split(gathered), split(w_msg[...]))

    with scope("D_takeA"):
        take_vals(0)
    def at_inner(steps):
        @pl.when(inner)
        def _():
            for step, u, j in steps:
                step(u, j, True) if step is not finish_sum else step(u, j)

    def at_outer(steps):
        if nz > 2:

            @pl.when(outer)
            def _():
                for step, u, j in steps:
                    step(u, j, False)

    def sums(h):
        for j in range(nz):
            partial_sums(h, j)
            x_copy(h, j).start()
            if j > 1:
                at_outer([(send_sum, 2 * h, j - 2)])
        at_outer([(send_sum, 2 * h, j) for j in range(max(nz - 2, 0), nz)])
        at_outer([(send_sum, 2 * h + 1, j) for j in range(nz)])

    S, F, T = send_sum, finish_sum, take_filtered
    rest = list(range(1, side_z))

    def early(step, u):
        return [(step, u, 0 if step is not finish_sum else side_z)]

    def late(step, u):
        return [(step, u, j if step is not finish_sum else side_z + j) for j in rest]

    def own(u):
        return [(T, u, side_z)]

    def own_late(u):
        return [(T, u, side_z + j) for j in rest]

    cut = 1 + (plane - 1) // 3, 1 + 2 * (plane - 1) // 3

    with scope("D_psumA"):
        sums(0)
    with scope("D_send0"):
        at_inner(early(S, 0) + late(S, 0))
    start_near()
    with scope("E_takeB"):
        take_vals(1)
    with scope("E_psumB"):
        sums(1)
    with scope("F_mid"):
        if nz > 2:

            @pl.when(inner)
            def _():
                filt_copy().wait_recv()

        at_inner(
            early(F, 0) + early(S, 1) + late(F, 0) + late(S, 1) + early(T, 0) + early(F, 1) + late(T, 0)
            + early(S, 2) + late(F, 1) + late(S, 2)
        )
        at_outer(own(0) + own_late(0) + early(T, 0) + own(1) + late(T, 0))
    for load in loads[5:8]:
        load.wait()
    if nz > 2:
        with scope("F_msg"):

            @pl.when(outer)
            def _():
                own_message()

    with scope("G_gather0"):
        gather(0)
    with scope("G_back0"):
        back_range(0, 1, cut[1])
    with scope("G_a"):
        at_inner(early(T, 1) + early(F, 2) + late(T, 1) + early(S, 3) + late(F, 2) + late(S, 3))
        at_outer(own_late(1))
    with scope("G_back0"):
        back_range(0, cut[1], plane)
    with scope("G_b"):
        at_outer(early(T, 1) + own(2) + late(T, 1))
    with scope("G_gather1"):
        gather(1)
    with scope("G_back1"):
        back_range(1, 1, cut[0])
    with scope("G_c"):
        at_inner(early(T, 2) + early(F, 3) + late(T, 2) + late(F, 3))
        at_outer(own_late(2))
    with scope("G_back1"):
        back_range(1, cut[0], plane)
    with scope("G_d"):
        at_outer(early(T, 2) + own(3) + late(T, 2))
    with scope("G_gather2"):
        gather(2)
    with scope("G_back2"):
        back_range(2, 1, cut[0])
    with scope("G_e"):
        at_inner(early(T, 3))
    with scope("G_back2"):
        back_range(2, cut[0], cut[1])
    with scope("G_f"):
        at_inner(late(T, 3))
    with scope("G_back2"):
        back_range(2, cut[1], plane)
    with scope("K_take"):
        at_outer(own_late(3) + early(T, 3) + late(T, 3))
    with scope("K_msg"):

        @pl.when(inner)
        def _():
            own_message()

    with scope("K_gather3"):
        gather(3)
    with scope("K_back3"):
        back_range(3, 1, plane)
    with scope("K_own"):
        for u in range(pieces):
            back(u, 0)

    with scope("M_ewait"):
        for u in range(pieces):

            @pl.loop(1, plane)
            def _(j):
                e_copy(u, j).wait_recv()
                es[u, 0] = es[u, 0] + er[u, j]

    with scope("N_mlp"):
        summed = msg[...] + jnp.concatenate([es[u, 0] for u in range(pieces)], axis=0).T
        normed = summed / jnp.sqrt(jnp.mean(summed * summed, axis=1, keepdims=True) + 1e-06)
        v = dot3(split(normed), split(w_one[...]))
        hidden = v / (1.0 + jnp.exp(-v))
        result = summed + dot3(split(hidden), split(w_two[...]))
        for c in range(cells):
            part = slice(c * cell, (c + 1) * cell)
            out[part, :] = jnp.where(slot_ids < counts[c], result[part], 0.0)

    _sc = scope("O_waits")
    _sc.__enter__()
    for j in range(1, nz):
        kv_copy(j).wait_send()
    for j in range(nz):
        for h in range(2):
            x_copy(h, j).wait_send()
        for u in range(pieces):
            zb = block_at(j)
            f_relay(u, zb).wait_send()
            if j < side_z:
                s_hop(u, j, 0).wait_send()
            elif nz > 2:

                @pl.when(outer)
                def _():
                    s_hop(u, j, 0).wait_send()

            @pl.when(inner)
            def _():
                if nz > 2:
                    f_hop(u, zb, 1, away).wait_send()
                if j >= side_z:
                    f_hop(u, zb, 0, toward).wait_send()

    if nz > 2:

        @pl.when(outer)
        def _():
            filt_copy().wait_send()

    @pl.loop(1, plane)
    def _(j):
        pos_copy(j).wait_send()
        val_copy(1, j).wait_send()
        for u in range(pieces):
            e_copy(u, j).wait_send()

    for side, there in ((0, jnp.logical_not(at_high)), (1, jnp.logical_not(at_low))):

        @pl.when(there)
        def _():
            for copy in near_copies(side):
                copy.wait_send()

    @pl.when(at_edge)
    def _():
        for copy in via_copies() + on_copies():
            copy.wait_send()

    _sc.__exit__(None, None, None)


def shards(
    nz, feats, positions, cell_counts, neighbours, nbr_count, kvec, filters, w_msg, w_val, w_one, w_two
):
    slots, width = feats.shape
    kb = kvec.shape[1]
    waves = lax.axis_size("waves")
    plane = waves // nz
    devices = lax.axis_size("rows") * waves
    kpad = -(-nz * kb // 128) * 128
    kbpad = -(-kb // 128) * 128
    half = kb // 2
    hw = width // 2
    scale = 1.0 / math.sqrt(float(slots * devices) * float(kb * waves))
    natoms = plane * slots
    vm = pltpu.VMEM
    dma = pltpu.SemaphoreType.DMA
    any_spec = pl.BlockSpec(memory_space=pl.ANY)
    vmem_spec = pl.BlockSpec(memory_space=pltpu.VMEM)
    return pl.pallas_call(
        functools.partial(body, nz, plane, scale),
        out_shape=pltpu.VMEM((slots, width), F32),
        in_specs=[any_spec] * 11,
        out_specs=vmem_spec,
        scratch_shapes=[
            pltpu.SMEM(cell_counts.shape, jnp.int32),
            pltpu.SMEM(neighbours.shape, jnp.int32),
            pltpu.SMEM(nbr_count.shape, jnp.int32),
            vm((slots, width), F32),
            vm((3, slots), F32),
            vm((3, kb), F32),
            vm((kb, width), F32),
            vm((width, width), F32),
            vm((width, width), F32),
            vm((width, width), F32),
            vm((width, width), F32),
            vm((slots, width), F32),
            vm((8, slots), F32),
            vm((8, kbpad), F32),
            vm((2, slots, hw), F32),
            vm((2, plane, slots, hw), F32),
            vm((plane, 8, slots), F32),
            vm((nz, 8, kbpad), F32),
            vm((2, slots, width), F32),
            vm((2, 8, slots), F32),
            vm((slots, width), F32),
            vm((8, slots), F32),
            vm((kpad, 128), BF16),
            vm((kpad, natoms), BF16),
            vm((kpad, natoms), BF16),
            vm((kpad, natoms), BF16),
            vm((kpad, natoms), BF16),
            vm((2, natoms, width), BF16),
            vm((2, nz, 2, 2, half, hw), F32),
            vm((2, nz, 2, half, hw), F32),
            vm((4, nz, half, hw), F32),
            vm((2, 4, nz, half, hw), F32),
            vm((4, kpad, hw), F32),
            vm((4, 2, hw, kpad), BF16),
            vm((4, plane, hw // 2, slots), F32),
            vm((4, plane, hw // 2, slots), F32),
            vm((slots, width), F32),
            vm((half, width), F32),
            dma((11,)),
            dma((plane,)),
            dma((plane,)),
            dma((2, plane)),
            dma((2, plane)),
            dma((2, 2)),
            dma((2, 2)),
            dma((2,)),
            dma((2,)),
            dma((2,)),
            dma((nz,)),
            dma((nz,)),
            dma((2, nz)),
            dma((2, nz)),
            dma((4, nz)),
            dma((2, 4, nz)),
            dma((4, nz, 2)),
            dma((4, nz, 2)),
            dma((4, nz)),
            dma((4, plane)),
            dma((4, plane)),
            dma((1,)),
            dma((1,)),
        ],
        compiler_params=pltpu.CompilerParams(collective_id=0, has_side_effects=True),
        name="ewald_layer",
    )(cell_counts, neighbours, nbr_count, feats, positions, kvec, filters, w_msg, w_val, w_one, w_two)


def solution(mesh):
    nz = 4 if mesh.shape["waves"] % 4 == 0 else 2
    placed = (
        P(("rows", "waves"), None),
        P(None, ("rows", "waves")),
        P(("rows", "waves")),
        P(("rows", "waves"), None),
        P(("rows", "waves")),
        P(None, "waves"),
        P("waves", None),
        P(),
        P(),
        P(),
        P(),
    )
    return jax.shard_map(
        functools.partial(shards, nz),
        mesh=mesh,
        in_specs=placed,
        out_specs=P(("rows", "waves"), None),
        check_vma=False,
    )
```

time: 69.1 us -> 53.6 us (0.78)
  Pallas kernels: 67.3 us -> 52.7 us
  local copies, waits for them, and re-layouts: 1.67 us -> 0.71 us
    pallas_call x1, Pallas kernels: 67.3 us -> 52.7 us  [shards(): pl.pallas_call(functools.partial(body, nz, plane, scale), out_shape=pltpu...]
    unnamed x1, local copies, waits for them, and re-layouts: 1.67 us -> 0.71 us
where the time goes in v2:
time: 53.6 us; the launch traced here: 53.4 us
  Pallas kernels  52.7 us (98%)
  local copies, waits for them, and re-layouts  0.71 us (1%)
    pallas_call x1, Pallas kernels, shards(): pl.pallas_call(functools.partial(body, nz, plane, scale), out_shape=pltpu...  52.7 us

profile of v2, /device:TPU:0, one launch (start us, length us, event | category | flops | bytes accessed | tf_op | source)
XLA Modules:
  0.0 53.4 jit_solution(6678942599159744501)
XLA Ops:
  0.0 52.7 %ewald_layer.1 = f32[256,256]{1,0:T(8,128)S(1)} custom-call(s32[2]{0:T(128)} %counts_in.1, s32[2,5]{1,0:T(2,128)} %neigh_in.1, s32[2]{0:T(128)} %ncount_in.1, f32[256,256]{1,0:T(8,128)} %feats_in.1, f32[3,256]{1,0:T(4,128)} %pos_in.1, f32[3,192]{1,0:T(4,128)} %kv_in.1, f32[192,256]{1,0:T(8,128)} %filt_in.1, f32[256,256]{1,0:T(8,128)} %w_msg_in.1, ...), custom_call_target="tpu_custom_call" | custom-call | tf_op jit(solution)/shard_map/ewald_layer/pallas_call | solution.py:674
  52.7 0.7 %copy.13 = f32[256,256]{1,0:T(8,128)} copy(f32[256,256]{1,0:T(8,128)S(1)} %ewald_layer.1) | data formatting | bytes 524288

commit v3 on v2

--- a/solution.py
+++ b/solution.py
@@ -60,10 +60,10 @@
     nz, plane, scale,
     counts_in, neigh_in, ncount_in, feats_in, pos_in, kv_in, filt_in, w_msg_in, w_val_in, w_one_in, w_two_in,
     out,
-    counts, neigh, ncount, feats, pos3, kv3, filt, w_msg, w_val, w_one, w_two,
-    fm, pos, kv, vals, vals_all, pos_all, kv_all, near_feat, near_pos, via_feat, via_pos, km, ch, cl, sh, sl, fcat,
+    counts, neigh, ncount, feats, pos3, kv3, filt, w_val, w_late,
+    fm, pos, kv, vals, vals_all, pos_all, kv_all, near, via, km, ch, cl, sh, sl, fcat,
     s_acc, xbuf, zs, zr, f_all, ft, es, er, msg, filt_far,
-    s_in, s_pos, r_pos, s_val, r_val, s_near, r_near, s_via, r_via, s_on, s_kv, r_kv, s_x, r_x, s_z, r_z, s_f, r_f, s_g, s_e, r_e, s_filt, r_filt,
+    s_in, s_late, s_pos, r_pos, s_val, r_val, s_near, r_near, s_via, r_via, s_on, s_kv, r_kv, s_x, r_x, s_z, r_z, s_f, r_f, s_g, r_g, s_e, r_e, s_filt, r_filt,
 ):
     slots, width = feats.shape
     kb = filt.shape[0]
@@ -93,6 +93,17 @@
     def plane_dev(j):
         return (r, z * plane + (p + j) % plane)
 
+    bits = (plane - 1).bit_length()
+
+    def peer(j):
+        q = p
+        for b in range(bits):
+            q = q + ((j // (1 << b)) % 2) * (1 << b) * (1 - 2 * ((p // (1 << b)) % 2))
+        return q
+
+    def peer_dev(j):
+        return (r, z * plane + peer(j))
+
     def z_dev(j):
         return (r, ((z + j) % nz) * plane + p)
 
@@ -113,16 +124,16 @@
                 (feats_in, feats),
                 (w_val_in, w_val),
                 (filt_in, filt),
-                (w_msg_in, w_msg),
-                (w_one_in, w_one),
-                (w_two_in, w_two),
                 (counts_in, counts),
                 (neigh_in, neigh),
                 (ncount_in, ncount),
             )
         )
     ]
-    for load in loads:
+    late_loads = [
+        pltpu.make_async_copy(src, w_late.at[i], s_late) for i, src in enumerate((w_msg_in, w_one_in, w_two_in))
+    ]
+    for load in loads + late_loads:
         load.start()
 
     natoms = plane * slots
@@ -162,94 +173,91 @@
         pos[0:3, :] = pos3[...]
         kv[...] = jnp.zeros_like(kv)
         kv[0:3, 0:kb] = kv3[...] * (0.5 / math.pi)
+    with scope("A_barrier"):
+        pl.semaphore_wait(barrier, nz + plane - 1 + jnp.where(met, 1, 0))
+
+    def kv_copy(j):
+        return rcopy(kv, kv_all.at[z], s_kv, r_kv.at[z], z_dev(j))
+
+    def kv_arrival(j):
+        q = (z + j) % nz
+        return rcopy(kv, kv_all.at[q], s_kv, r_kv.at[q], z_dev(j))
+
+    def pos_copy(j):
+        return rcopy(pos, pos_all.at[p], s_pos, r_pos, peer_dev(j))
+
+    def val_copy(h, j):
+        return rcopy(vals.at[h], vals_all.at[h, p], s_val.at[h], r_val.at[h], peer_dev(j))
+
+    def all_pos():
+        block = pos_all.at[pl.ds(0, plane - 1)]
+        return rcopy(block, block, s_pos, r_pos, other)
+
+    def all_vals(h):
+        block = vals_all.at[h, pl.ds(0, plane - 1)]
+        return rcopy(block, block, s_val.at[h], r_val.at[h], other)
+
+    def near_copy(side):
+        dev = plane_dev(1 if side == 0 else plane - 1)
+        return rcopy(fm, near.at[side], s_near.at[side], r_near.at[side], dev)
+
+    def via_copy():
+        dev = (r, ((z + jnp.where(at_high, 1, nz - 1)) % nz) * plane + p)
+        return rcopy(fm, via, s_via, r_via, dev)
+
+    def on_copy():
+        side = jnp.where(at_high, 0, 1)
+        flip = (at_high & (z == 0)) | (at_low & (z == nz - 1))
+        dev = (jnp.where(flip, 1 - r, r), facing)
+        return rcopy(via, near.at[side], s_on, r_near.at[side], dev)
+
+    def start_near():
+        for side, there in ((0, jnp.logical_not(at_high)), (1, jnp.logical_not(at_low))):
+
+            @pl.when(there)
+            def _():
+                near_copy(side).start()
+
+    def start_on():
+        @pl.when(at_edge)
+        def _():
+            via_copy().wait_recv()
+            on_copy().start()
+
+    def filt_copy():
+        return rcopy(filt.at[pl.ds(mine, half), :], filt_far, s_filt.at[0], r_filt.at[0], toward)
+
+    for j in range(1, nz):
+        kv_copy(j).start()
+
+    @pl.loop(1, plane)
+    def _(j):
+        pos_copy(j).start()
+
+    slot_ids = lax.broadcasted_iota(jnp.int32, (cell, width), 0)
+    with scope("B_project"):
         loads[2].wait()
-        for load in loads[8:]:
+        for load in loads[5:]:
             load.wait()
-        slot_ids = lax.broadcasted_iota(jnp.int32, (cell, width), 0)
         for c in range(cells):
             part = slice(c * cell, (c + 1) * cell)
             fm[part, :] = jnp.where(slot_ids < counts[c], feats[part, :], 0.0)
+        fm[slots:, 0:slots] = pos[...]
         loads[3].wait()
-        projected = dot3(split(fm[...]), split(w_val[...]))
+        projected = dot3(split(fm[0:slots, :]), split(w_val[...]))
         for h in range(2):
             vals[h] = projected[:, h * hw : (h + 1) * hw]
 
+    @pl.loop(1, plane)
+    def _(j):
+        val_copy(0, plane - j).start()
+
     loads[4].wait()
-    with scope("A_barrier"):
-        pl.semaphore_wait(barrier, nz + plane - 1 + jnp.where(met, 1, 0))
-
-    def kv_copy(j):
-        return rcopy(kv, kv_all.at[z], s_kv.at[j], r_kv.at[z], z_dev(j))
-
-    def kv_arrival(j):
-        q = (z + j) % nz
-        return rcopy(kv, kv_all.at[q], s_kv.at[j], r_kv.at[q], z_dev(j))
-
-    def pos_copy(j):
-        return rcopy(pos, pos_all.at[p], s_pos.at[j], r_pos.at[p], plane_dev(j))
-
-    def pos_arrival(q):
-        return rcopy(pos, pos_all.at[q], s_pos.at[0], r_pos.at[q], other)
-
-    def val_copy(h, j):
-        return rcopy(vals.at[h], vals_all.at[h, p], s_val.at[h, j], r_val.at[h, p], plane_dev(j))
-
-    def val_arrival(h, q):
-        return rcopy(vals.at[h], vals_all.at[h, q], s_val.at[h, 0], r_val.at[h, q], other)
-
-    def pair(feat_src, pos_src, feat_dst, pos_dst, ssem, rsem, dev):
-        return (
-            rcopy(pos_src, pos_dst, ssem.at[0], rsem.at[0], dev),
-            rcopy(feat_src, feat_dst, ssem.at[1], rsem.at[1], dev),
-        )
-
-    def near_copies(side):
-        dev = plane_dev(1 if side == 0 else plane - 1)
-        return pair(fm, pos, near_feat.at[side], near_pos.at[side], s_near.at[side], r_near.at[side], dev)
-
-    def via_copies():
-        dev = (r, ((z + jnp.where(at_high, 1, nz - 1)) % nz) * plane + p)
-        return pair(fm, pos, via_feat, via_pos, s_via, r_via, dev)
-
-    def on_copies():
-        side = jnp.where(at_high, 0, 1)
-        flip = (at_high & (z == 0)) | (at_low & (z == nz - 1))
-        dev = (jnp.where(flip, 1 - r, r), facing)
-        return pair(via_feat, via_pos, near_feat.at[side], near_pos.at[side], s_on, r_near.at[side], dev)
-
-    def start_near():
-        for side, there in ((0, jnp.logical_not(at_high)), (1, jnp.logical_not(at_low))):
-
-            @pl.when(there)
-            def _():
-                for copy in near_copies(side):
-                    copy.start()
-
-        @pl.when(at_edge)
-        def _():
-            for arrived, copy in zip(via_copies(), on_copies()):
-                arrived.wait_recv()
-                copy.start()
-
-    def filt_copy():
-        return rcopy(filt.at[pl.ds(mine, half), :], filt_far, s_filt.at[0], r_filt.at[0], toward)
-
-    for j in range(1, nz):
-        kv_copy(j).start()
-
     if nz > 2:
 
         @pl.when(outer)
         def _():
             filt_copy().start()
-
-    @pl.loop(1, plane)
-    def _(j):
-        pos_copy(j).start()
-
-    @pl.loop(1, plane)
-    def _(j):
-        val_copy(0, j).start()
 
     def place_k(block, rows):
         a, b, c = split3(rows)
@@ -276,8 +284,7 @@
 
                 @pl.when(at_edge)
                 def _():
-                    for copy in via_copies():
-                        copy.start()
+                    via_copy().start()
 
             q = (z + j) % nz
             place_k(q, kv_all[q])
@@ -300,25 +307,24 @@
 
         @pl.loop(0, plane)
         def _(j):
-            q = (p + j) % plane
-
-            @pl.when(j > 0)
+            q = peer(j)
+
+            @pl.when(j == 1)
             def _():
                 with scope("c_poswait"):
-                    pos_arrival(q).wait_recv()
+                    all_pos().wait_recv()
 
             with scope("c_phase"):
                 phases(q, pos_all[q])
 
             @pl.when(j == plane // 2)
             def _():
+                all_vals(0).wait_send()
+
                 @pl.loop(1, plane)
                 def _(k):
-                    val_copy(0, k).wait_send()
-
-                @pl.loop(1, plane)
-                def _(k):
-                    val_copy(1, k).start()
+                    val_copy(1, plane - k).start()
+
 
     def partial_sums(h, j):
         zb = block_at(j)
@@ -334,62 +340,77 @@
 
     def x_copy(h, j):
         zb = block_at(j)
-        return rcopy(s_acc.at[h, zb, 1 - r], xbuf.at[h, zb], s_x.at[h, zb], r_x.at[h, zb], other)
-
-    def s_hop(u, j, source):
+        return rcopy(s_acc.at[h, zb, 1 - r], xbuf.at[h, zb], s_x, r_x.at[h, zb], other)
+
+    def units(u):
+        if u < pieces - 1 or half % 16:
+            return [(u, slice(0, half))]
+        return [(u, slice(0, half // 2)), (u + 1, slice(half // 2, half))]
+
+    def s_hop(u, j, source, unit):
         zb = block_at(j)
-        return rcopy(zs.at[u, zb], zr.at[source, u, zb], s_z.at[u, zb], r_z.at[source, u, zb], toward)
-
-    def gathered_sum(u, j, sources):
+        index, rows = unit
+        return rcopy(zs.at[u, zb, rows], zr.at[source, u, zb, rows], s_z, r_f.at[index, zb] if source else r_z.at[index, zb], toward)
+
+    def gathered_sum(u, j, sources, unit):
         zb = block_at(j)
+        rows = unit[1]
+        total = s_acc[u // 2, zb, r, u % 2, rows, :] + xbuf[u // 2, zb, u % 2, rows, :]
+        for source in sources:
+            s_hop(u, j, source, unit).wait_recv()
+            total = total + zr[source, u, zb, rows, :]
+        return total
+
+    def send_sum(u, j, is_inner):
         if u % 2 == 0:
             x_copy(u // 2, j).wait_recv()
-        total = s_acc[u // 2, zb, r, u % 2] + xbuf[u // 2, zb, u % 2]
-        for source in sources:
-            s_hop(u, j, source).wait_recv()
-            total = total + zr[source, u, zb]
-        return total
-
-    def send_sum(u, j, is_inner):
-        zs[u, block_at(j)] = gathered_sum(u, j, (0,) if is_inner and nz > 2 else ())
-        s_hop(u, j, 1 if is_inner else 0).start()
-
-    def share(u, zb, c):
-        return f_all.at[u, pl.ds(pl.multiple_of((zb * 2 + c) * half, 8), half), :]
-
-    def f_hop(u, zb, way, dev):
-        here = share(u, zb, r)
-        return rcopy(here, here, s_f.at[u, zb, way], r_f.at[u, zb, r], dev)
-
-    def f_relay(u, zb):
-        here = share(u, zb, r)
-        return rcopy(here, here, s_g.at[u, zb], r_f.at[u, zb, r], other)
-
-    def f_arrival(u, zb, c):
-        here = share(u, zb, c)
-        return rcopy(here, here, s_g.at[u, zb], r_f.at[u, zb, c], other)
+        for unit in units(u):
+            zs[u, block_at(j), unit[1], :] = gathered_sum(u, j, (0,) if is_inner and nz > 2 else (), unit)
+            s_hop(u, j, 1 if is_inner else 0, unit).start()
+
+    def share(u, zb, rows):
+        start = pl.multiple_of((zb * 2 + r) * half + rows.start, 8)
+        return f_all.at[u, pl.ds(start, rows.stop - rows.start), :]
+
+    def f_hop(u, zb, way, dev, unit):
+        here = share(u, zb, unit[1])
+        return rcopy(here, here, s_f.at[way], r_f.at[unit[0], zb], dev)
+
+    def f_relay(u, zb, unit):
+        here = share(u, zb, unit[1])
+        return rcopy(here, here, s_g, r_g.at[u], other)
+
+    def filtered_bytes(pieces_sent, ssem, rsem):
+        block = f_all.at[pl.ds(0, pieces_sent), pl.ds(0, nz * half)]
+        return rcopy(block, block, ssem, rsem, other)
 
     def finish_sum(u, j):
         zb = block_at(j)
         lanes = slice(u * qw, (u + 1) * qw)
-        rows = filt[pl.ds(mine, half), lanes] if j == nz - 1 else filt_far[:, lanes]
-        rows = jnp.concatenate([rows, rows], axis=1) * scale
-        total = gathered_sum(u, j, (0, 1) if nz > 2 else (1,))
-        f_all[u, pl.ds(pl.multiple_of((zb * 2 + r) * half, 8), half), :] = rows * total
-        if nz > 2:
-            f_hop(u, zb, 1, away).start()
-        f_hop(u, zb, 0, toward).start()
-        f_relay(u, zb).start()
+        kept = filt[pl.ds(mine, half), lanes] if j == nz - 1 else filt_far[:, lanes]
+        kept = jnp.concatenate([kept, kept], axis=1) * scale
+        if u % 2 == 0:
+            x_copy(u // 2, j).wait_recv()
+        for unit in units(u):
+            rows = unit[1]
+            total = gathered_sum(u, j, (0, 1) if nz > 2 else (1,), unit)
+            start = pl.multiple_of((zb * 2 + r) * half + rows.start, 8)
+            f_all[u, pl.ds(start, rows.stop - rows.start), :] = kept[rows] * total
+            f_hop(u, zb, 0, toward, unit).start()
+            if nz > 2:
+                f_hop(u, zb, 1, away, unit).start()
+            f_relay(u, zb, unit).start()
 
     def take_filtered(u, j, is_inner):
         zb = block_at(j)
-        f_arrival(u, zb, r).wait_recv()
-        if is_inner and nz > 2:
-            f_hop(u, zb, 1, away).start()
-        f_relay(u, zb).start()
+        for unit in units(u):
+            f_hop(u, zb, 0, other, unit).wait_recv()
+            if is_inner and nz > 2:
+                f_hop(u, zb, 1, away, unit).start()
+            f_relay(u, zb, unit).start()
 
     def back(u, j):
-        lanes = rows_of((p + j) % plane)
+        lanes = rows_of(peer(j))
         total = jnp.zeros((qw, slots), F32)
         for part, (hi, lo) in enumerate(((ch, cl), (sh, sl))):
             both = mm(ft[u, part], hi[:, lanes])
@@ -397,11 +418,14 @@
         es[u, j] = total
 
     def e_copy(u, j):
-        return rcopy(es.at[u, j], er.at[u, j], s_e.at[u, j], r_e.at[u, j], plane_dev(j))
+        return rcopy(es.at[u, j], er.at[u, j], s_e, r_e.at[u // (pieces - 1)], peer_dev(j))
+
+    def all_e(start, stop, group):
+        block = er.at[pl.ds(start, stop - start), pl.ds(1, plane - 1)]
+        return rcopy(block, block, s_e, r_e.at[group], other)
 
     def gather(u):
-        for zb in range(nz):
-            f_arrival(u, zb, 1 - r).wait_recv()
+        filtered_bytes(1, s_g, r_g.at[u]).wait_recv()
         a, b = split(f_all[u].T)
         for part in range(2):
             rows = slice(part * qw, (part + 1) * qw)
@@ -410,15 +434,17 @@
 
     def back_range(u, start, stop):
         @pl.loop(start, stop)
-        def _(j):
+        def _(k):
+            j = plane - k
             back(u, j)
             e_copy(u, j).start()
 
     def take_vals(h):
+        all_vals(h).wait_recv()
+
         @pl.loop(1, plane)
         def _(j):
-            q = (p + j) % plane
-            val_arrival(h, q).wait_recv()
+            q = peer(j)
             place_v(h, q, vals_all[h, q])
 
     def own_message():
@@ -441,13 +467,13 @@
         gathered = jnp.zeros((slots, width), F32)
         for shift in (-1, 0, 1):
             if shift:
-                for copy in near_copies(0 if shift < 0 else 1):
-                    copy.wait_recv()
-            near = pos[...] if shift == 0 else near_pos[0 if shift < 0 else 1]
-            atoms = fm[...] if shift == 0 else near_feat[0 if shift < 0 else 1]
+                near_copy(0 if shift < 0 else 1).wait_recv()
+            block = fm if shift == 0 else near.at[0 if shift < 0 else 1]
+            where = block[slots:, 0:slots]
+            atoms = block[0:slots, :]
             dist = jnp.zeros((slots, slots), F32)
             for axis in range(3):
-                diff = own_cols[:, axis : axis + 1] - near[axis : axis + 1]
+                diff = own_cols[:, axis : axis + 1] - where[axis : axis + 1]
                 dist = dist + diff * diff
             live = jnp.zeros((slots, slots), F32)
             for c in range(cells):
@@ -458,7 +484,7 @@
             if shift == 0:
                 weight = jnp.where(same, 0.0, weight)
             gathered = gathered + dot3(split(weight), split(atoms))
-        msg[...] = feats[...] + 0.125 * dot3(split(gathered), split(w_msg[...]))
+        msg[...] = feats[...] + 0.125 * dot3(split(gathered), split(w_late[0]))
 
     with scope("D_takeA"):
         take_vals(0)
@@ -476,12 +502,14 @@
                 for step, u, j in steps:
                     step(u, j, False)
 
-    def sums(h):
+    def sums(h, then=()):
         for j in range(nz):
             partial_sums(h, j)
             x_copy(h, j).start()
             if j > 1:
                 at_outer([(send_sum, 2 * h, j - 2)])
+            if j == nz // 2 - 1:
+                at_inner(then)
         at_outer([(send_sum, 2 * h, j) for j in range(max(nz - 2, 0), nz)])
         at_outer([(send_sum, 2 * h + 1, j) for j in range(nz)])
 
@@ -505,12 +533,13 @@
     with scope("D_psumA"):
         sums(0)
     with scope("D_send0"):
-        at_inner(early(S, 0) + late(S, 0))
+        at_inner(early(S, 0))
     start_near()
+    start_on()
     with scope("E_takeB"):
         take_vals(1)
     with scope("E_psumB"):
-        sums(1)
+        sums(1, late(S, 0))
     with scope("F_mid"):
         if nz > 2:
 
@@ -523,8 +552,7 @@
             + early(S, 2) + late(F, 1) + late(S, 2)
         )
         at_outer(own(0) + own_late(0) + early(T, 0) + own(1) + late(T, 0))
-    for load in loads[5:8]:
-        load.wait()
+    pltpu.make_async_copy(w_late, w_late, s_late).wait()
     if nz > 2:
         with scope("F_msg"):
 
@@ -583,72 +611,59 @@
             back(u, 0)
 
     with scope("M_ewait"):
-        for u in range(pieces):
-
-            @pl.loop(1, plane)
-            def _(j):
-                e_copy(u, j).wait_recv()
-                es[u, 0] = es[u, 0] + er[u, j]
+        for start, stop, group in ((0, pieces - 1, 0), (pieces - 1, pieces, 1)):
+            all_e(start, stop, group).wait_recv()
+            for u in range(start, stop):
+
+                @pl.loop(1, plane)
+                def _(j):
+                    es[u, 0] = es[u, 0] + er[u, j]
 
     with scope("N_mlp"):
         summed = msg[...] + jnp.concatenate([es[u, 0] for u in range(pieces)], axis=0).T
         normed = summed / jnp.sqrt(jnp.mean(summed * summed, axis=1, keepdims=True) + 1e-06)
-        v = dot3(split(normed), split(w_one[...]))
+        v = dot3(split(normed), split(w_late[1]))
         hidden = v / (1.0 + jnp.exp(-v))
-        result = summed + dot3(split(hidden), split(w_two[...]))
+        result = summed + dot3(split(hidden), split(w_late[2]))
         for c in range(cells):
             part = slice(c * cell, (c + 1) * cell)
             out[part, :] = jnp.where(slot_ids < counts[c], result[part], 0.0)
 
     _sc = scope("O_waits")
     _sc.__enter__()
-    for j in range(1, nz):
-        kv_copy(j).wait_send()
-    for j in range(nz):
-        for h in range(2):
-            x_copy(h, j).wait_send()
-        for u in range(pieces):
-            zb = block_at(j)
-            f_relay(u, zb).wait_send()
-            if j < side_z:
-                s_hop(u, j, 0).wait_send()
-            elif nz > 2:
-
-                @pl.when(outer)
-                def _():
-                    s_hop(u, j, 0).wait_send()
-
-            @pl.when(inner)
-            def _():
-                if nz > 2:
-                    f_hop(u, zb, 1, away).wait_send()
-                if j >= side_z:
-                    f_hop(u, zb, 0, toward).wait_send()
+    block = kv_all.at[pl.ds(0, nz - 1)]
+    rcopy(block, block, s_kv, r_kv.at[0], other).wait_send()
+    all_pos().wait_send()
+    all_vals(1).wait_send()
+    rcopy(s_acc.at[:, :, 0], xbuf, s_x, r_x.at[0, 0], other).wait_send()
+    filtered_bytes(pieces, s_g, r_g.at[0]).wait_send()
+    all_e(0, pieces, 0).wait_send()
+
+    @pl.when(inner)
+    def _():
+        block = zs.at[:, pl.ds(0, side_z)]
+        rcopy(block, block, s_z, r_z.at[0, 0], other).wait_send()
+        filtered_bytes(pieces * side_z // nz, s_f.at[0], r_f.at[0, 0]).wait_send()
+        if nz > 2:
+            filtered_bytes(pieces, s_f.at[1], r_f.at[0, 0]).wait_send()
 
     if nz > 2:
 
         @pl.when(outer)
         def _():
+            rcopy(zs, zs, s_z, r_z.at[0, 0], other).wait_send()
             filt_copy().wait_send()
-
-    @pl.loop(1, plane)
-    def _(j):
-        pos_copy(j).wait_send()
-        val_copy(1, j).wait_send()
-        for u in range(pieces):
-            e_copy(u, j).wait_send()
 
     for side, there in ((0, jnp.logical_not(at_high)), (1, jnp.logical_not(at_low))):
 
         @pl.when(there)
         def _():
-            for copy in near_copies(side):
-                copy.wait_send()
+            near_copy(side).wait_send()
 
     @pl.when(at_edge)
     def _():
-        for copy in via_copies() + on_copies():
-            copy.wait_send()
+        via_copy().wait_send()
+        on_copy().wait_send()
 
     _sc.__exit__(None, None, None)
 
@@ -685,20 +700,16 @@
             vm((3, kb), F32),
             vm((kb, width), F32),
             vm((width, width), F32),
-            vm((width, width), F32),
-            vm((width, width), F32),
-            vm((width, width), F32),
-            vm((slots, width), F32),
+            vm((3, width, width), F32),
+            vm((slots + 8, width), F32),
             vm((8, slots), F32),
             vm((8, kbpad), F32),
             vm((2, slots, hw), F32),
             vm((2, plane, slots, hw), F32),
             vm((plane, 8, slots), F32),
             vm((nz, 8, kbpad), F32),
-            vm((2, slots, width), F32),
-            vm((2, 8, slots), F32),
-            vm((slots, width), F32),
-            vm((8, slots), F32),
+            vm((2, slots + 8, width), F32),
+            vm((slots + 8, width), F32),
             vm((kpad, 128), BF16),
             vm((kpad, natoms), BF16),
             vm((kpad, natoms), BF16),
@@ -715,27 +726,29 @@
             vm((4, plane, hw // 2, slots), F32),
             vm((slots, width), F32),
             vm((half, width), F32),
-            dma((11,)),
-            dma((plane,)),
-            dma((plane,)),
-            dma((2, plane)),
-            dma((2, plane)),
-            dma((2, 2)),
-            dma((2, 2)),
+            dma((8,)),
+            dma(()),
+            dma(()),
+            dma(()),
             dma((2,)),
             dma((2,)),
             dma((2,)),
+            dma((2,)),
+            dma(()),
+            dma(()),
+            dma(()),
+            dma(()),
             dma((nz,)),
-            dma((nz,)),
+            dma(()),
             dma((2, nz)),
-            dma((2, nz)),
-            dma((4, nz)),
-            dma((2, 4, nz)),
-            dma((4, nz, 2)),
-            dma((4, nz, 2)),
-            dma((4, nz)),
-            dma((4, plane)),
-            dma((4, plane)),
+            dma(()),
+            dma((5, nz)),
+            dma((2,)),
+            dma((5, nz)),
+            dma(()),
+            dma((4,)),
+            dma(()),
+            dma((2,)),
             dma((1,)),
             dma((1,)),
         ],

time: 53.6 us -> 52.6 us (0.981)
  Pallas kernels: 52.7 us -> 51.7 us
    pallas_call x1, Pallas kernels: 52.7 us -> 51.7 us  [shards(): pl.pallas_call(functools.partial(body, nz, plane, scale), out_shape=pltpu...]
where the time goes in v3:
time: 52.6 us; the launch traced here: 52.4 us
  Pallas kernels  51.7 us (98%)
  local copies, waits for them, and re-layouts  0.71 us (1%)
    pallas_call x1, Pallas kernels, shards(): pl.pallas_call(functools.partial(body, nz, plane, scale), out_shape=pltpu...  51.7 us

profile of v3, /device:TPU:0, one launch (start us, length us, event | category | flops | bytes accessed | tf_op | source)
XLA Modules:
  0.0 52.4 jit_solution(2137404289809026768)
XLA Ops:
  0.0 51.7 %ewald_layer.1 = f32[256,256]{1,0:T(8,128)S(1)} custom-call(s32[2]{0:T(128)} %counts_in.1, s32[2,5]{1,0:T(2,128)} %neigh_in.1, s32[2]{0:T(128)} %ncount_in.1, f32[256,256]{1,0:T(8,128)} %feats_in.1, f32[3,256]{1,0:T(4,128)} %pos_in.1, f32[3,192]{1,0:T(4,128)} %kv_in.1, f32[192,256]{1,0:T(8,128)} %filt_in.1, f32[256,256]{1,0:T(8,128)} %w_msg_in.1, ...), custom_call_target="tpu_custom_call" | custom-call | tf_op jit(solution)/shard_map/ewald_layer/pallas_call | solution.py:689
  51.7 0.7 %copy.13 = f32[256,256]{1,0:T(8,128)} copy(f32[256,256]{1,0:T(8,128)S(1)} %ewald_layer.1) | data formatting | bytes 524288

commit v4 on v3

--- a/solution.py
+++ b/solution.py
@@ -62,7 +62,7 @@
     out,
     counts, neigh, ncount, feats, pos3, kv3, filt, w_val, w_late,
     fm, pos, kv, vals, vals_all, pos_all, kv_all, near, via, km, ch, cl, sh, sl, fcat,
-    s_acc, xbuf, zs, zr, f_all, ft, es, er, msg, filt_far,
+    s_acc, xbuf, zs, zr, f_all, ft, es, er, msg, filt_far, w_split,
     s_in, s_late, s_pos, r_pos, s_val, r_val, s_near, r_near, s_via, r_via, s_on, s_kv, r_kv, s_x, r_x, s_z, r_z, s_f, r_f, s_g, r_g, s_e, r_e, s_filt, r_filt,
 ):
     slots, width = feats.shape
@@ -548,8 +548,7 @@
                 filt_copy().wait_recv()
 
         at_inner(
-            early(F, 0) + early(S, 1) + late(F, 0) + late(S, 1) + early(T, 0) + early(F, 1) + late(T, 0)
-            + early(S, 2) + late(F, 1) + late(S, 2)
+            early(F, 0) + early(S, 1) + late(F, 0) + late(S, 1) + early(T, 0) + early(F, 1) + early(S, 2) + late(T, 0) + late(F, 1) + late(S, 2)
         )
         at_outer(own(0) + own_late(0) + early(T, 0) + own(1) + late(T, 0))
     pltpu.make_async_copy(w_late, w_late, s_late).wait()
@@ -565,7 +564,7 @@
     with scope("G_back0"):
         back_range(0, 1, cut[1])
     with scope("G_a"):
-        at_inner(early(T, 1) + early(F, 2) + late(T, 1) + early(S, 3) + late(F, 2) + late(S, 3))
+        at_inner(early(T, 1) + early(F, 2) + early(S, 3) + late(T, 1) + late(F, 2) + late(S, 3))
         at_outer(own_late(1))
     with scope("G_back0"):
         back_range(0, cut[1], plane)
@@ -606,25 +605,35 @@
         gather(3)
     with scope("K_back3"):
         back_range(3, 1, plane)
+    final = pieces - 1
     with scope("K_own"):
         for u in range(pieces):
             back(u, 0)
-
+        for i in range(2):
+            for k, piece in enumerate(split(w_late[i + 1])):
+                w_split[i, k] = piece
+
+    def add_arrivals(u):
+        @pl.loop(1, plane)
+        def _(j):
+            es[u, 0] = es[u, 0] + er[u, j]
+
+    with scope("M_pre"):
+        all_e(0, final, 0).wait_recv()
+        for u in range(final):
+            add_arrivals(u)
+        msg[:, 0:hw] = msg[:, 0:hw] + jnp.concatenate([es[0, 0], es[1, 0]], axis=0).T
     with scope("M_ewait"):
-        for start, stop, group in ((0, pieces - 1, 0), (pieces - 1, pieces, 1)):
-            all_e(start, stop, group).wait_recv()
-            for u in range(start, stop):
-
-                @pl.loop(1, plane)
-                def _(j):
-                    es[u, 0] = es[u, 0] + er[u, j]
+        all_e(final, pieces, 1).wait_recv()
+        add_arrivals(final)
 
     with scope("N_mlp"):
-        summed = msg[...] + jnp.concatenate([es[u, 0] for u in range(pieces)], axis=0).T
+        right = msg[:, hw:width] + jnp.concatenate([es[2, 0], es[3, 0]], axis=0).T
+        summed = jnp.concatenate([msg[:, 0:hw], right], axis=1)
         normed = summed / jnp.sqrt(jnp.mean(summed * summed, axis=1, keepdims=True) + 1e-06)
-        v = dot3(split(normed), split(w_late[1]))
+        v = dot3(split(normed), (w_split[0, 0], w_split[0, 1]))
         hidden = v / (1.0 + jnp.exp(-v))
-        result = summed + dot3(split(hidden), split(w_late[2]))
+        result = summed + dot3(split(hidden), (w_split[1, 0], w_split[1, 1]))
         for c in range(cells):
             part = slice(c * cell, (c + 1) * cell)
             out[part, :] = jnp.where(slot_ids < counts[c], result[part], 0.0)
@@ -726,6 +735,7 @@
             vm((4, plane, hw // 2, slots), F32),
             vm((slots, width), F32),
             vm((half, width), F32),
+            vm((2, 2, width, width), BF16),
             dma((8,)),
             dma(()),
             dma(()),

time: 52.6 us -> 52.5 us (level)
  no operation moved by 1% of the time
where the time goes in v4:
time: 52.5 us; the launch traced here: 52.3 us
  Pallas kernels  51.6 us (98%)
  local copies, waits for them, and re-layouts  0.71 us (1%)
    pallas_call x1, Pallas kernels, shards(): pl.pallas_call(functools.partial(body, nz, plane, scale), out_shape=pltpu...  51.6 us

profile of v4, /device:TPU:0, one launch (start us, length us, event | category | flops | bytes accessed | tf_op | source)
XLA Modules:
  0.0 52.3 jit_solution(12122294968933806764)
XLA Ops:
  0.0 51.6 %ewald_layer.1 = f32[256,256]{1,0:T(8,128)S(1)} custom-call(s32[2]{0:T(128)} %counts_in.1, s32[2,5]{1,0:T(2,128)} %neigh_in.1, s32[2]{0:T(128)} %ncount_in.1, f32[256,256]{1,0:T(8,128)} %feats_in.1, f32[3,256]{1,0:T(4,128)} %pos_in.1, f32[3,192]{1,0:T(4,128)} %kv_in.1, f32[192,256]{1,0:T(8,128)} %filt_in.1, f32[256,256]{1,0:T(8,128)} %w_msg_in.1, ...), custom_call_target="tpu_custom_call" | custom-call | tf_op jit(solution)/shard_map/ewald_layer/pallas_call | solution.py:698
  51.6 0.7 %copy.13 = f32[256,256]{1,0:T(8,128)} copy(f32[256,256]{1,0:T(8,128)S(1)} %ewald_layer.1) | data formatting | bytes 524288
